TPU v7x, 512 devices: a whole 4x8x8 slice. The times are simulated.
512 devices in a mesh: dom: 128 (over z, y, x_hi), off: 4 (over x_lo, core).
Axes of the slice: x: 4 (x_hi: 2, x_lo: 2; x = x_hi * 2 + x_lo), y: 8, z: 8, core: 2. Of those that a mesh axis runs over, the one named last changes fastest.
Arguments:
- contrib: float32 [3072, 2432], P('dom'), may hold values from -6 to 6
- slot_octant: int32 [3072], P('dom'), may hold values from 0 to 2047, as said below
- vlist_src: int32 [2048, 80], P('dom'), may hold values from 0 to 2047, as said below
- vlist_class: int32 [2048, 80], P('dom'), may hold values from 0 to 159, as said below
- translation: float32 [160, 152, 152], P('off'), may hold values from -0.0546875 to 0.0546875
Outputs:
- potential: float32 [2048, 2432], P(('dom', 'off'))
Inputs may be any that keep to these rules, and one draw needn't show every extreme that they name: `slot_octant`: slot k < 16 of partition p names octant p * 16 + k; its other slots name octants p * 16 + j with -4 <= j < 20, taken modulo 2048, and each partition has one slot at j = -4 and one at j = 19. vlist_src[t, l] = t + d modulo 2048, where the nonzero offset d, with |d| <= 12, depends only on the class vlist_class[t, l]; some class has d = 12 and some d = -12. `vlist_class`: the 80 classes of one octant are all different, and every class is used by some octant.
All inputs are finite; a program needn't handle non-finite values.
Results may differ from a plain program's by a relative error of at most 0.00007.
Values sent between devices are 32-bit elements; how exact they have to be, the bound alone decides.
A program may use at most 64 MiB of HBM per device.

v0:
```python
import jax
import jax.numpy as jnp
from jax import lax
from jax.sharding import PartitionSpec as P

E = 152
R = 16
TGT = 16
SPILL = 4


class_group = 8


def padded(block, sides, width):
    for axis, dim in sides:
        count = lax.axis_size(axis)
        forward = [(i, i + 1) for i in range(count - 1)]
        forward.append((count - 1, 0))
        backward = [(target, source) for source, target in forward]
        low = lax.ppermute(
            lax.slice_in_dim(block, block.shape[dim] - width, None, axis=dim), axis, forward
        )
        high = lax.ppermute(lax.slice_in_dim(block, 0, width, axis=dim), axis, backward)
        block = jnp.concatenate([low, block, high], axis=dim)
    return block


def over_pieces(array, axis):
    return lax.all_gather(array, axis).sum(0)


def spread_rows(local_ids, values, count):
    columns = jnp.arange(count)
    onehot = (local_ids[:, None] == columns[None, :]).astype(jnp.float32)
    return jnp.dot(
        onehot.T, values, precision=lax.Precision.HIGHEST, preferred_element_type=jnp.float32
    )


def local(contrib, slot_octant, vlist_src, vlist_class, translation):
    octants = TGT * lax.axis_size("dom")
    reach = TGT - SPILL
    position = lax.axis_index("dom")
    first_octant = position * TGT - SPILL
    local_ids = (slot_octant - first_octant + octants) % octants
    table = spread_rows(local_ids, contrib, TGT + 2 * SPILL)
    widened = padded(table, (("dom", 0),), TGT)
    lower = widened[:TGT]
    middle = widened[TGT : 2 * TGT + 2 * SPILL]
    upper = widened[2 * TGT + 2 * SPILL :]
    window = jnp.pad(lower, ((0, 2 * TGT - 2 * SPILL), (0, 0)))
    window = window + jnp.pad(middle, ((TGT - 2 * SPILL, TGT - 2 * SPILL), (0, 0)))
    window = window + jnp.pad(upper, ((2 * TGT - 2 * SPILL, 0), (0, 0)))
    window_start = position * TGT - reach
    window_ids = (vlist_src - window_start + octants) % octants
    targets = vlist_src.shape[0]
    class_count = translation.shape[0]
    first_class = lax.axis_index("off") * class_count

    def class_block(running, block_index):
        classes = first_class + block_index * class_group + jnp.arange(class_group, dtype=jnp.int32)
        matches = vlist_class[:, :, None] == classes[None, None, :]
        chosen = jnp.max(jnp.where(matches, window_ids[:, :, None], -1), axis=1)
        present = (chosen >= 0).astype(jnp.float32)
        sources = window[jnp.maximum(chosen, 0)] * present[:, :, None]
        sources = sources.reshape(targets, class_group, E, R)
        blocks = lax.dynamic_slice_in_dim(translation, block_index * class_group, class_group, 0)
        running = running + jnp.einsum(
            "cij,tcjr->tir", blocks, sources, precision=lax.Precision.HIGHEST
        )
        return (running, None)

    running, ignored = lax.scan(
        class_block,
        jnp.zeros((targets, E, R), jnp.float32),
        jnp.arange(class_count // class_group, dtype=jnp.int32),
    )
    partial_sum = running.reshape(targets, E * R)
    whole = over_pieces(partial_sum, "off")
    share = targets // lax.axis_size("off")
    return lax.dynamic_slice_in_dim(whole, lax.axis_index("off") * share, share, 0)


def solution(mesh):
    return jax.shard_map(
        local,
        mesh=mesh,
        in_specs=(P("dom", None), P("dom"), P("dom", None), P("dom", None), P("off", None, None)),
        out_specs=P(("dom", "off"), None),
        check_vma=False,
    )
```

profile of v0, /device:TPU:1, one launch (start us, length us, event | category | flops | bytes accessed | tf_op | source)
XLA Modules:
  0.0 171.5 jit_solution(17333444851886250610)
XLA Ops:
  0.0 0.0 copy-start
  0.0 0.7 and_select_fusion
  0.7 0.2 copy-done
  1.0 0.4 fusion.16
  1.4 5.5 %collective-permute-start = (f32[16,2432]{1,0:T(8,128)S(1)}, f32[16,2432]{1,0:T(8,128)S(1)}, u32[]{:S(2)}, u32[]{:S(2)}) collective-permute-start(f32[16,2432]{1,0:T(8,128)S(1)} %get-tuple-element.91), channel_id=1, source_target_pairs={{0,4},{4,8},{8,12},{12,16},{16,20},{20,24},{24,28},{28,32},{32,36}... | collective-permute-start | bytes 466952 | tf_op jit(solution)/shard_map/ppermute | solution.py:21
  6.8 13.3 %collective-permute-start.1 = (f32[16,2432]{1,0:T(8,128)S(1)}, f32[16,2432]{1,0:T(8,128)S(1)}, u32[]{:S(2)}, u32[]{:S(2)}) collective-permute-start(f32[16,2432]{1,0:T(8,128)S(1)} %get-tuple-element.92), channel_id=1, source_target_pairs={{4,0},{8,4},{12,8},{16,12},{20,16},{24,20},{28,24},{32,28},{36,32}... | collective-permute-start | bytes 466952 | tf_op jit(solution)/shard_map/ppermute | solution.py:24
  20.2 0.7 add_select_fusion
  20.9 1.1 collective-permute-done
  21.9 0.9 collective-permute-done.1
  22.9 138.9 %while.11 = (s32[]{:T(128)}, f32[16,152,16]{1,2,0:T(8,128)S(1)}, s32[16,80]{1,0:T(8,128)}, s32[5]{0:T(128)S(1)}, s32[]{:T(128)}, /*index=5*/s32[16,80]{1,0:T(8,1...) while((s32[]{:T(128)}, f32[16,152,16]{1,2,0:T(8,128)S(1)}, ...), condition=%wide.region_2.3_spmd.clone, body=%wide.region_0.2_spmd.clone.sunk | while | flops 568225024 | bytes 16518413 | solution.py:74
  22.9 0.7 dynamic_slice.25
  24.3 1.1 select_reduce_fusion.2
  25.4 0.1 reshape.45
  25.5 1.1 gather_fusion
  26.6 5.4 %gather.12 = f32[16,8,152,16]{3,2,1,0:T(8,128)} reshape(f32[128,2432]{1,0:T(8,128)S(1)} %gather_fusion) | data formatting | bytes 2490368 | tf_op jit(solution)/shard_map/while/body/eval_jaxpr/gather | solution.py:66
  32.0 18.7 %fusion.27 = f32[16,152,16]{1,2,0:T(8,128)S(1)} fusion(f32[40,152,152]{2,1,0:T(8,128)} %get-tuple-element.173, s32[]{:T(128)S(6)} %select_n.35, f32[16,8,152,16]{3,2,1,0:T(8,128)} %gather.12, f32[16,8]{1,0:T(8,128)S(1)} %compare_convert_fusion.2, f32[16,152,16]{1,2,0:T(8,128)S(1)} %get-tuple-element.155, pred[]{:T(512)S(6)} %compare.8), kind=kOutput, calls=%fused_computation.7.clone.1 | convolution fusion | flops 568193024 | bytes 11518469 | tf_op jit(solution)/shard_map/while/body/eval_jaxpr/cij,tcjr->tir/dot_general | solution.py:69
  50.7 0.7 dynamic_slice.25
  52.1 1.1 select_reduce_fusion.2
  53.2 0.1 reshape.45
  53.3 1.1 gather_fusion
  54.4 5.4 %gather.12 = f32[16,8,152,16]{3,2,1,0:T(8,128)} reshape(f32[128,2432]{1,0:T(8,128)S(1)} %gather_fusion) | data formatting | bytes 2490368 | tf_op jit(solution)/shard_map/while/body/eval_jaxpr/gather | solution.py:66
  59.8 18.7 %fusion.27 = f32[16,152,16]{1,2,0:T(8,128)S(1)} fusion(f32[40,152,152]{2,1,0:T(8,128)} %get-tuple-element.173, s32[]{:T(128)S(6)} %select_n.35, f32[16,8,152,16]{3,2,1,0:T(8,128)} %gather.12, f32[16,8]{1,0:T(8,128)S(1)} %compare_convert_fusion.2, f32[16,152,16]{1,2,0:T(8,128)S(1)} %get-tuple-element.155, pred[]{:T(512)S(6)} %compare.8), kind=kOutput, calls=%fused_computation.7.clone.1 | convolution fusion | flops 568193024 | bytes 11518469 | tf_op jit(solution)/shard_map/while/body/eval_jaxpr/cij,tcjr->tir/dot_general | solution.py:69
  78.5 0.7 dynamic_slice.25
  79.9 1.1 select_reduce_fusion.2
  81.0 0.1 reshape.45
  81.1 1.1 gather_fusion
  82.2 5.4 %gather.12 = f32[16,8,152,16]{3,2,1,0:T(8,128)} reshape(f32[128,2432]{1,0:T(8,128)S(1)} %gather_fusion) | data formatting | bytes 2490368 | tf_op jit(solution)/shard_map/while/body/eval_jaxpr/gather | solution.py:66
  87.6 18.7 %fusion.27 = f32[16,152,16]{1,2,0:T(8,128)S(1)} fusion(f32[40,152,152]{2,1,0:T(8,128)} %get-tuple-element.173, s32[]{:T(128)S(6)} %select_n.35, f32[16,8,152,16]{3,2,1,0:T(8,128)} %gather.12, f32[16,8]{1,0:T(8,128)S(1)} %compare_convert_fusion.2, f32[16,152,16]{1,2,0:T(8,128)S(1)} %get-tuple-element.155, pred[]{:T(512)S(6)} %compare.8), kind=kOutput, calls=%fused_computation.7.clone.1 | convolution fusion | flops 568193024 | bytes 11518469 | tf_op jit(solution)/shard_map/while/body/eval_jaxpr/cij,tcjr->tir/dot_general | solution.py:69
  106.3 0.7 dynamic_slice.25
  107.6 1.1 select_reduce_fusion.2
  108.8 0.1 reshape.45
  108.9 1.1 gather_fusion
  110.0 5.4 %gather.12 = f32[16,8,152,16]{3,2,1,0:T(8,128)} reshape(f32[128,2432]{1,0:T(8,128)S(1)} %gather_fusion) | data formatting | bytes 2490368 | tf_op jit(solution)/shard_map/while/body/eval_jaxpr/gather | solution.py:66
  115.4 18.7 %fusion.27 = f32[16,152,16]{1,2,0:T(8,128)S(1)} fusion(f32[40,152,152]{2,1,0:T(8,128)} %get-tuple-element.173, s32[]{:T(128)S(6)} %select_n.35, f32[16,8,152,16]{3,2,1,0:T(8,128)} %gather.12, f32[16,8]{1,0:T(8,128)S(1)} %compare_convert_fusion.2, f32[16,152,16]{1,2,0:T(8,128)S(1)} %get-tuple-element.155, pred[]{:T(512)S(6)} %compare.8), kind=kOutput, calls=%fused_computation.7.clone.1 | convolution fusion | flops 568193024 | bytes 11518469 | tf_op jit(solution)/shard_map/while/body/eval_jaxpr/cij,tcjr->tir/dot_general | solution.py:69
  134.0 0.7 dynamic_slice.25
  135.4 1.1 select_reduce_fusion.2
  136.6 0.1 reshape.45
  136.7 1.1 gather_fusion
  137.7 5.4 %gather.12 = f32[16,8,152,16]{3,2,1,0:T(8,128)} reshape(f32[128,2432]{1,0:T(8,128)S(1)} %gather_fusion) | data formatting | bytes 2490368 | tf_op jit(solution)/shard_map/while/body/eval_jaxpr/gather | solution.py:66
  143.2 18.7 %fusion.27 = f32[16,152,16]{1,2,0:T(8,128)S(1)} fusion(f32[40,152,152]{2,1,0:T(8,128)} %get-tuple-element.173, s32[]{:T(128)S(6)} %select_n.35, f32[16,8,152,16]{3,2,1,0:T(8,128)} %gather.12, f32[16,8]{1,0:T(8,128)S(1)} %compare_convert_fusion.2, f32[16,152,16]{1,2,0:T(8,128)S(1)} %get-tuple-element.155, pred[]{:T(512)S(6)} %compare.8), kind=kOutput, calls=%fused_computation.7.clone.1 | convolution fusion | flops 568193024 | bytes 11518469 | tf_op jit(solution)/shard_map/while/body/eval_jaxpr/cij,tcjr->tir/dot_general | solution.py:69
  161.8 0.4 copy.12
  162.2 0.4 all_gather_reshape.3
  162.6 8.2 %all_gather.3 = f32[4,16,2432]{2,1,0:T(8,128)S(1)} all-gather(f32[1,16,2432]{2,1,0:T(8,128)S(1)} %all_gather_reshape.3), channel_id=1, replica_groups=mesh['dom'=128,'off'=4] {'off'}, dimensions={0}, use_global_device_ids=true | all-gather | bytes 778240 | tf_op jit(solution)/shard_map/all_gather | solution.py:30
  170.8 0.6 constant_dynamic-slice_fusion
  (25 shorter events, 0.2 us)
Async XLA Ops:
  0.0 1.0 copy-start
  1.4 20.6 %collective-permute-start = (f32[16,2432]{1,0:T(8,128)S(1)}, f32[16,2432]{1,0:T(8,128)S(1)}, u32[]{:S(2)}, u32[]{:S(2)}) collective-permute-start(f32[16,2432]{1,0:T(8,128)S(1)} %get-tuple-element.91), channel_id=1, source_target_pairs={{0,4},{4,8},{8,12},{12,16},{16,20},{20,24},{24,28},{28,32},{32,36}... | collective-permute-start | bytes 466952 | tf_op jit(solution)/shard_map/ppermute | solution.py:21
  6.8 16.0 %collective-permute-start.1 = (f32[16,2432]{1,0:T(8,128)S(1)}, f32[16,2432]{1,0:T(8,128)S(1)}, u32[]{:S(2)}, u32[]{:S(2)}) collective-permute-start(f32[16,2432]{1,0:T(8,128)S(1)} %get-tuple-element.92), channel_id=1, source_target_pairs={{4,0},{8,4},{12,8},{16,12},{20,16},{24,20},{28,24},{32,28},{36,32}... | collective-permute-start | bytes 466952 | tf_op jit(solution)/shard_map/ppermute | solution.py:24
where the time goes:
time: 172 us; the launch traced here: 171 us
  matrix products  93.7 us (54%)
  local copies, waits for them, and re-layouts  37.9 us (22%)
  starting transfers between devices  18.8 us (11%)
  blocking collectives  8.17 us (5%)
  other arithmetic  7.12 us (4%)
  loops' own time  3.83 us (2%)
  waiting for transfers between devices  1.96 us (1%)
    dot_general x5, matrix products, class_block(): jnp.einsum('cij,tcjr->tir', blocks, sources, precision=lax.Precision.HIGH...  93.3 us
    gather x10, local copies, waits for them, and re-layouts, class_block(): sources = window[jnp.maximum(chosen, 0)] * present[:, :, None]  32.4 us
    ppermute x1, starting transfers between devices, padded(): lax.ppermute(lax.slice_in_dim(block, 0, width, axis=dim), axis, backward)  13.3 us
    all_gather x1, blocking collectives, over_pieces(): return lax.all_gather(array, axis).sum(0)  8.17 us
    reduce_max x5, other arithmetic, class_block(): chosen = jnp.max(jnp.where(matches, window_ids[:, :, None], -1), axis=1)  5.54 us
    ppermute x1, starting transfers between devices, padded(): lax.ppermute(lax.slice_in_dim(block, block.shape[dim] - width, None, axis...  5.47 us
    another operation x1, loops' own time, local(): lax.scan(class_block, jnp.zeros((targets, E, R), jnp.float32), jnp.arange...  3.83 us
  transfers between devices with their start and end apart: 2, of which 2 were waited for; matrix products, arithmetic and copies ran while one was open for 0% of the time, Pallas kernels for 0%

commit v1 on v0

v1 whole, which is shorter than its diff:
```python
import jax
import jax.numpy as jnp
from jax import lax
from jax.experimental import pallas as pl
from jax.experimental.pallas import tpu as pltpu
from jax.sharding import PartitionSpec as P

MESH = pl.DeviceIdType.MESH
E = 152
R = 16
TGT = 16
SPILL = 4
REACH = TGT - SPILL
SLOTS = 24
LANES = 128
EP = 160
HALF = EP // 2
TILES = 20
OFFS = 4
GROUP = 8


def block_transpose(v):
    row = lax.broadcasted_iota(jnp.int32, (8, LANES), 0)
    blk = lax.broadcasted_iota(jnp.int32, (8, LANES), 1) // R
    v = jnp.where(
        ((row ^ blk) & 4) == 0, v, pltpu.roll(pltpu.roll(v, 4, 0), LANES // 2, 1)
    )
    for b in (2, 1):
        above = pltpu.roll(pltpu.roll(v, b, 0), LANES - R * b, 1)
        below = pltpu.roll(pltpu.roll(v, 8 - b, 0), R * b, 1)
        moved = jnp.where((row & b) != 0, above, below)
        v = jnp.where(((row ^ blk) & b) == 0, v, moved)
    return v


def split(x):
    hi = x.astype(jnp.bfloat16)
    lo = (x - hi.astype(jnp.float32)).astype(jnp.bfloat16)
    return hi, lo


def kernel(
    parts,
    contrib_ref, slot_ref, src_ref, cls_ref, trans_ref, out_ref,
    cbuf, slots, srcv, clsv, traw, tpack,
    own, halo, yhi, ylo, offs, masks, codes, codes_s,
    sendbuf, recvbuf,
    load_sem, trans_sem, halo_send, halo_recv, fwd_send, fwd_recv, code_sem, rs_send, rs_recv,
):
    dom = lax.axis_index("dom")
    off = lax.axis_index("off")
    core = lax.rem(off, 2)
    octants = TGT * parts
    classes = trans_ref.shape[0]
    groups = classes // GROUP
    left = (lax.rem(dom + parts - 1, parts), lax.rem(off + 2, OFFS))
    right = (lax.rem(dom + 1, parts), lax.rem(off + 2, OFFS))
    mate = (dom, off + 1 - 2 * core)

    barrier = pltpu.get_barrier_semaphore()
    peers = [left, right] + [(dom, lax.rem(off + n, OFFS)) for n in (1, 2, 3)]
    for peer in peers:
        pl.semaphore_signal(barrier, inc=1, device_id=peer, device_id_type=MESH)

    loads = [
        pltpu.make_async_copy(contrib_ref, cbuf.at[:, pl.ds(0, E * R)], load_sem.at[0]),
        pltpu.make_async_copy(slot_ref, slots, load_sem.at[1]),
        pltpu.make_async_copy(src_ref, srcv, load_sem.at[2]),
        pltpu.make_async_copy(cls_ref, clsv, load_sem.at[3]),
    ]
    for copy in loads:
        copy.start()

    def trans_copy(g):
        rows = pl.ds(g * GROUP, GROUP)
        return pltpu.make_async_copy(trans_ref.at[rows], traw.at[rows], trans_sem.at[g])

    for g in range(groups):
        trans_copy(g).start()

    cbuf[:, pl.ds(E * R, LANES)] = jnp.zeros((SLOTS, LANES), jnp.float32)
    row = lax.broadcasted_iota(jnp.int32, (8, LANES), 0)
    loads[0].wait()
    loads[1].wait()
    ids = [
        lax.rem(slots[TGT + s] - (dom * TGT - SPILL) + octants, octants)
        for s in range(SLOTS - TGT)
    ]

    @pl.loop(0, TILES // 2)
    def _(pair):
        for half in range(2):
            g = pair * 2 + half
            lanes = pl.ds(pl.multiple_of(g * LANES, LANES), LANES)
            first = pltpu.roll(cbuf[pl.ds(0, 8), lanes], 4, 0)
            second = pltpu.roll(cbuf[pl.ds(8, 8), lanes], 4, 0)
            table = [
                jnp.where(row >= 4, first, 0.0),
                jnp.where(row < 4, first, second),
                jnp.where(row < 4, second, 0.0),
            ]
            for s in range(SLOTS - TGT):
                spill = jnp.broadcast_to(cbuf[pl.ds(TGT + s, 1), lanes], (8, LANES))
                for b in range(3):
                    table[b] = table[b] + jnp.where(row + 8 * b == ids[s], spill, 0.0)
            for b in range(3):
                own[pl.ds(pl.multiple_of(g * 8, 8), 8), pl.ds(b * LANES, LANES)] = (
                    block_transpose(table[b])
                )

    pl.semaphore_wait(barrier, len(peers))

    half_rows = pl.ds(pl.multiple_of(core * HALF, HALF), HALF)
    sends = []
    for n, (peer, lane) in enumerate(((right, LANES), (left, 0))):
        copy = pltpu.make_async_remote_copy(
            src_ref=own.at[half_rows, pl.ds(lane, 2 * LANES)],
            dst_ref=halo.at[n, half_rows],
            send_sem=halo_send.at[n],
            recv_sem=halo_recv.at[n],
            device_id=peer,
            device_id_type=MESH,
        )
        copy.start()
        sends.append(copy)

    loads[2].wait()
    loads[3].wait()
    target = lax.broadcasted_iota(jnp.int32, srcv.shape, 0) + dom * TGT
    code = lax.rem(srcv[...] - target + (REACH + octants), octants) + 1
    spread = (
        lax.broadcasted_iota(jnp.int32, (TGT, TGT * R), 0)
        == lax.broadcasted_iota(jnp.int32, (TGT, TGT * R), 1) // R
    ).astype(jnp.float32)
    dims = (((0,), (0,)), ((), ()))
    code_l = lax.dot_general(
        code.astype(jnp.float32), spread, dims, preferred_element_type=jnp.float32
    )
    class_l = lax.dot_general(
        (clsv[...] - off * classes).astype(jnp.float32), spread, dims,
        preferred_element_type=jnp.float32,
    )

    @pl.loop(0, classes)
    def _(c):
        found = jnp.max(
            jnp.where(class_l == c.astype(jnp.float32), code_l, 0.0), axis=0, keepdims=True
        )
        offs[pl.ds(c, 1), :] = found
        present = jnp.broadcast_to((found > 0.0).astype(jnp.float32), (16, TGT * R))
        masks[c] = present.astype(jnp.bfloat16)

    start = jnp.max(offs[...], axis=1, keepdims=True).astype(jnp.int32) - 1
    codes[...] = jnp.broadcast_to(jnp.clip(start, 0, 2 * REACH), codes.shape)
    code_copy = pltpu.make_async_copy(codes, codes_s, code_sem)
    code_copy.start()

    @pl.loop(0, groups)
    def _(g):
        trans_copy(g).wait()
        for m in range(GROUP):
            hi, lo = split(traw[g * GROUP + m])
            tpack[g * GROUP + m, pl.ds(0, E), :] = hi
            tpack[g * GROUP + m, pl.ds(EP, E), :] = lo

    code_copy.wait()

    forwards = []
    for n in range(2):
        sends[n].wait_recv()
        copy = pltpu.make_async_remote_copy(
            src_ref=halo.at[n, half_rows],
            dst_ref=halo.at[n, half_rows],
            send_sem=fwd_send.at[n],
            recv_sem=fwd_recv.at[n],
            device_id=mate,
            device_id_type=MESH,
        )
        copy.start()
        forwards.append(copy)
    for copy in forwards:
        copy.wait_recv()

    lane16 = lax.broadcasted_iota(jnp.int32, (16, LANES), 1)

    @pl.loop(0, EP // 16)
    def _(b):
        rows = pl.ds(pl.multiple_of(b * 16, 16), 16)

        def tile(ref, q):
            return ref[rows, pl.ds(q * LANES, LANES)]

        lhalo, rhalo = halo.at[0], halo.at[1]
        window = [
            tile(lhalo, 0),
            tile(lhalo, 1) + tile(own, 0),
            tile(own, 1),
            tile(own, 2) + tile(rhalo, 0),
            tile(rhalo, 1),
        ]
        for s in range(8):
            shift = LANES - R * s
            if s == 0:
                tiles = window
            else:
                rolled = [pltpu.roll(w, shift, 1) for w in window]
                tiles = [jnp.where(lane16 < shift, rolled[q], rolled[q + 1]) for q in range(4)]
            for q, value in enumerate(tiles):
                hi, lo = split(value)
                yhi[s * 5 + q, rows, :] = hi
                ylo[s * 5 + q, rows, :] = lo

    def step(c, acc):
        begin = codes_s[c, 0]
        at = lax.rem(begin, 8) * 5 + begin // 8
        mask = masks[c]

        def sources(ref):
            pieces = [
                (ref[at + n].reshape(EP // 16, 16, LANES) * mask[None, :, n * LANES : (n + 1) * LANES])
                .reshape(EP, LANES)
                for n in range(2)
            ]
            return jnp.concatenate(pieces, axis=1)[:E]

        both = jnp.dot(tpack[c], sources(yhi), preferred_element_type=jnp.float32)
        low = jnp.dot(tpack[c, pl.ds(0, EP), :], sources(ylo), preferred_element_type=jnp.float32)
        return acc + (both[:EP] + (both[EP:] + low))

    acc = lax.fori_loop(0, classes, step, jnp.zeros((EP, TGT * R), jnp.float32))

    lane8 = lax.broadcasted_iota(jnp.int32, (8, LANES), 1)
    for g in range(TILES // 2):
        for h in range(2):
            a, b = (
                acc[(2 * g + n) * 8 : (2 * g + n + 1) * 8, h * LANES : (h + 1) * LANES]
                for n in range(2)
            )
            rows = pl.ds(g * 8, 8)
            sendbuf[2 * h, rows, :] = jnp.where(lane8 < 64, a, pltpu.roll(b, 64, 1))
            sendbuf[2 * h + 1, rows, :] = jnp.where(lane8 < 64, pltpu.roll(a, 64, 1), b)
    finals = []
    for n in (2, 3, 1):
        peer = lax.rem(off + n, OFFS)
        copy = pltpu.make_async_remote_copy(
            src_ref=sendbuf.at[peer],
            dst_ref=recvbuf.at[n],
            send_sem=rs_send.at[n - 1],
            recv_sem=rs_recv.at[n - 1],
            device_id=(dom, peer),
            device_id_type=MESH,
        )
        copy.start()
        finals.append(copy)
    for copy in finals:
        copy.wait_recv()
    for g in range(TILES // 2):
        rows = pl.ds(g * 8, 8)
        total = sendbuf[off, rows, :]
        for n in (1, 2, 3):
            total = total + recvbuf[n, rows, :]
        out_ref[:, pl.ds(2 * g * LANES, LANES)] = block_transpose(total)[: TGT // OFFS]
        if 2 * g + 1 < E // 8:
            other = block_transpose(pltpu.roll(total, 64, 1))
            out_ref[:, pl.ds((2 * g + 1) * LANES, LANES)] = other[: TGT // OFFS]
    for copy in sends + forwards + finals:
        copy.wait_send()


def solution(mesh):
    parts = mesh.shape["dom"]

    def local(contrib, slot_octant, vlist_src, vlist_class, translation):
        classes = translation.shape[0]
        wide = TGT * R
        any_spec = pl.BlockSpec(memory_space=pl.ANY)

        def body(*refs):
            kernel(parts, *refs)

        return pl.pallas_call(
            body,
            out_shape=jax.ShapeDtypeStruct((TGT // OFFS, E * R), jnp.float32),
            in_specs=[any_spec] * 5,
            out_specs=pl.BlockSpec(memory_space=pltpu.VMEM),
            scratch_shapes=[
                pltpu.VMEM((SLOTS, TILES * LANES), jnp.float32),
                pltpu.SMEM((SLOTS,), jnp.int32),
                pltpu.VMEM(vlist_src.shape, jnp.int32),
                pltpu.VMEM(vlist_class.shape, jnp.int32),
                pltpu.VMEM(translation.shape, jnp.float32),
                pltpu.VMEM((classes, 2 * EP, E), jnp.bfloat16),
                pltpu.VMEM((EP, 3 * LANES), jnp.float32),
                pltpu.VMEM((2, EP, 2 * LANES), jnp.float32),
                pltpu.VMEM((40, EP, LANES), jnp.bfloat16),
                pltpu.VMEM((40, EP, LANES), jnp.bfloat16),
                pltpu.VMEM((classes, wide), jnp.float32),
                pltpu.VMEM((classes, 16, wide), jnp.bfloat16),
                pltpu.VMEM((classes, LANES), jnp.int32),
                pltpu.SMEM((classes, LANES), jnp.int32),
                pltpu.VMEM((OFFS, HALF, LANES), jnp.float32),
                pltpu.VMEM((OFFS, HALF, LANES), jnp.float32),
                pltpu.SemaphoreType.DMA((4,)),
                pltpu.SemaphoreType.DMA((classes // GROUP,)),
                pltpu.SemaphoreType.DMA((2,)),
                pltpu.SemaphoreType.DMA((2,)),
                pltpu.SemaphoreType.DMA((2,)),
                pltpu.SemaphoreType.DMA((2,)),
                pltpu.SemaphoreType.DMA(()),
                pltpu.SemaphoreType.DMA((3,)),
                pltpu.SemaphoreType.DMA((3,)),
            ],
            compiler_params=pltpu.CompilerParams(collective_id=0, has_side_effects=True),
        )(contrib, slot_octant, vlist_src, vlist_class, translation)

    return jax.shard_map(
        local,
        mesh=mesh,
        in_specs=(P("dom", None), P("dom"), P("dom", None), P("dom", None), P("off", None, None)),
        out_specs=P(("dom", "off"), None),
        check_vma=False,
    )
```

time: 172 us -> 38.4 us (0.22)
  matrix products: 93.7 us -> 0 us
  Pallas kernels: 0 us -> 36.8 us
  local copies, waits for them, and re-layouts: 37.9 us -> 1.39 us
  starting transfers between devices: 18.8 us -> 0 us
  blocking collectives: 8.17 us -> 0 us
  other arithmetic: 7.12 us -> 0 us
  loops' own time: 3.83 us -> 0 us
  waiting for transfers between devices: 1.96 us -> 0 us
    dot_general x6 -> x0, matrix products: 93.7 us -> none  [the longest x5 93.3 us: class_block(): jnp.einsum('cij,tcjr->tir', blocks, sources, precision=lax.Precision.HIGH...]
    pallas_call x0 -> x1, Pallas kernels: none -> 36.8 us  [local(): pl.pallas_call(body, out_shape=jax.ShapeDtypeStruct((TGT // OFFS, E * R),...]
    gather x10 -> x0, local copies, waits for them, and re-layouts: 32.4 us -> none  [class_block(): sources = window[jnp.maximum(chosen, 0)] * present[:, :, None]]
    ppermute x2 -> x0, starting transfers between devices: 18.8 us -> none  [the longest x1 13.3 us: padded(): lax.ppermute(lax.slice_in_dim(block, 0, width, axis=dim), axis, backward)]
    all_gather x1 -> x0, blocking collectives: 8.17 us -> none  [over_pieces(): return lax.all_gather(array, axis).sum(0)]
    reduce_max x5 -> x0, other arithmetic: 5.54 us -> none  [class_block(): chosen = jnp.max(jnp.where(matches, window_ids[:, :, None], -1), axis=1)]
    dynamic_slice x6 -> x0, local copies, waits for them, and re-layouts: 3.97 us -> none  [the longest x5 3.33 us: local(): lax.scan(class_block, jnp.zeros((targets, E, R), jnp.float32), jnp.arange...]
    another operation x1 -> x0, loops' own time: 3.83 us -> none  [local(): lax.scan(class_block, jnp.zeros((targets, E, R), jnp.float32), jnp.arange...]
  transfers between devices with their start and end apart: 2 -> 0, of which waited for: 2 -> 0; matrix products, arithmetic and copies ran while one was open for 0% -> 0% of each run, Pallas kernels for 0% -> 0%
where the time goes in v1:
time: 38.4 us; the launch traced here: 38.2 us
  Pallas kernels  36.8 us (96%)
  local copies, waits for them, and re-layouts  1.39 us (4%)
    pallas_call x1, Pallas kernels, local(): pl.pallas_call(body, out_shape=jax.ShapeDtypeStruct((TGT // OFFS, E * R),...  36.8 us
    unnamed x1, local copies, waits for them, and re-layouts  1.39 us

profile of v1, /device:TPU:1, one launch (start us, length us, event | category | flops | bytes accessed | tf_op | source)
XLA Modules:
  0.0 38.2 jit_solution(15842794271821979964)
XLA Ops:
  0.0 36.8 %shard_map.55 = f32[4,2432]{1,0:T(4,128)} custom-call(f32[24,2432]{1,0:T(8,128)} %refs_0_.1, s32[24]{0:T(128)} %refs_1_.1, s32[16,80]{1,0:T(8,128)} %refs_2_.1, s32[16,80]{1,0:T(8,128)} %refs_3_.1, f32[40,152,152]{2,1,0:T(8,128)} %refs_4_.1), custom_call_target="tpu_custom_call" | custom-call | tf_op jit(solution)/shard_map/pallas_call | solution.py:282
  36.8 1.4 %copy.7 = f32[4,2432]{1,0:T(4,128)} copy(f32[4,2432]{1,0:T(4,128)} %shard_map.55) | data formatting | bytes 77824

commit v2 on v1

--- a/solution.py
+++ b/solution.py
@@ -18,6 +18,8 @@
 TILES = 20
 OFFS = 4
 GROUP = 8
+WIDE = TILES // 2 * LANES
+TAIL = EP - LANES
 
 
 def block_transpose(v):
@@ -51,23 +53,29 @@
     dom = lax.axis_index("dom")
     off = lax.axis_index("off")
     core = lax.rem(off, 2)
+    parity = lax.rem(dom, 2)
     octants = TGT * parts
     classes = trans_ref.shape[0]
     groups = classes // GROUP
-    left = (lax.rem(dom + parts - 1, parts), lax.rem(off + 2, OFFS))
-    right = (lax.rem(dom + 1, parts), lax.rem(off + 2, OFFS))
+    across = lax.rem(off + 2, OFFS)
     mate = (dom, off + 1 - 2 * core)
 
     barrier = pltpu.get_barrier_semaphore()
-    peers = [left, right] + [(dom, lax.rem(off + n, OFFS)) for n in (1, 2, 3)]
+    peers = [(lax.rem(dom + n, parts), across) for n in (1, parts - 1)]
+    peers += [(dom, lax.rem(off + n, OFFS)) for n in (1, 2, 3)]
     for peer in peers:
         pl.semaphore_signal(barrier, inc=1, device_id=peer, device_id_type=MESH)
 
+    def contrib_copy(start, size, sem):
+        lanes = pl.ds(pl.multiple_of(start, LANES), size)
+        return pltpu.make_async_copy(contrib_ref.at[:, lanes], cbuf.at[:, lanes], sem)
+
     loads = [
-        pltpu.make_async_copy(contrib_ref, cbuf.at[:, pl.ds(0, E * R)], load_sem.at[0]),
+        contrib_copy(core * (E * R - WIDE), WIDE, load_sem.at[0]),
         pltpu.make_async_copy(slot_ref, slots, load_sem.at[1]),
-        pltpu.make_async_copy(src_ref, srcv, load_sem.at[2]),
-        pltpu.make_async_copy(cls_ref, clsv, load_sem.at[3]),
+        contrib_copy((1 - core) * WIDE, E * R - WIDE, load_sem.at[2]),
+        pltpu.make_async_copy(src_ref, srcv, load_sem.at[3]),
+        pltpu.make_async_copy(cls_ref, clsv, load_sem.at[4]),
     ]
     for copy in loads:
         copy.start()
@@ -75,9 +83,6 @@
     def trans_copy(g):
         rows = pl.ds(g * GROUP, GROUP)
         return pltpu.make_async_copy(trans_ref.at[rows], traw.at[rows], trans_sem.at[g])
-
-    for g in range(groups):
-        trans_copy(g).start()
 
     cbuf[:, pl.ds(E * R, LANES)] = jnp.zeros((SLOTS, LANES), jnp.float32)
     row = lax.broadcasted_iota(jnp.int32, (8, LANES), 0)
@@ -88,11 +93,10 @@
         for s in range(SLOTS - TGT)
     ]
 
-    @pl.loop(0, TILES // 2)
-    def _(pair):
-        for half in range(2):
-            g = pair * 2 + half
-            lanes = pl.ds(pl.multiple_of(g * LANES, LANES), LANES)
+    def own_half(half):
+        for n in range(TILES // 2):
+            lanes = pl.ds(pl.multiple_of(half * WIDE, LANES) + n * LANES, LANES)
+            points = pl.ds(pl.multiple_of(half * HALF, 8) + n * 8, 8)
             first = pltpu.roll(cbuf[pl.ds(0, 8), lanes], 4, 0)
             second = pltpu.roll(cbuf[pl.ds(8, 8), lanes], 4, 0)
             table = [
@@ -105,28 +109,33 @@
                 for b in range(3):
                     table[b] = table[b] + jnp.where(row + 8 * b == ids[s], spill, 0.0)
             for b in range(3):
-                own[pl.ds(pl.multiple_of(g * 8, 8), 8), pl.ds(b * LANES, LANES)] = (
-                    block_transpose(table[b])
-                )
-
+                own[points, pl.ds(b * LANES, LANES)] = block_transpose(table[b])
+
+    own_half(core)
     pl.semaphore_wait(barrier, len(peers))
 
     half_rows = pl.ds(pl.multiple_of(core * HALF, HALF), HALF)
-    sends = []
-    for n, (peer, lane) in enumerate(((right, LANES), (left, 0))):
-        copy = pltpu.make_async_remote_copy(
-            src_ref=own.at[half_rows, pl.ds(lane, 2 * LANES)],
+
+    def halo_copy(n):
+        return pltpu.make_async_remote_copy(
+            src_ref=own.at[half_rows, pl.ds(pl.multiple_of((1 - n) * LANES, LANES), 2 * LANES)],
             dst_ref=halo.at[n, half_rows],
             send_sem=halo_send.at[n],
             recv_sem=halo_recv.at[n],
-            device_id=peer,
+            device_id=(lax.rem(dom + 1 + n * (parts - 2), parts), across),
             device_id_type=MESH,
         )
+
+    sends = [halo_copy(1 - parity), halo_copy(parity)]
+    for copy in sends:
         copy.start()
-        sends.append(copy)
-
+    for g in range(groups):
+        trans_copy(g).start()
     loads[2].wait()
+    own_half(1 - core)
+
     loads[3].wait()
+    loads[4].wait()
     target = lax.broadcasted_iota(jnp.int32, srcv.shape, 0) + dom * TGT
     code = lax.rem(srcv[...] - target + (REACH + octants), octants) + 1
     spread = (
@@ -156,20 +165,30 @@
     code_copy = pltpu.make_async_copy(codes, codes_s, code_sem)
     code_copy.start()
 
+    tpack[...] = jnp.zeros(tpack.shape, jnp.bfloat16)
+    pad = jnp.zeros((E, EP - E), jnp.float32)
+
     @pl.loop(0, groups)
     def _(g):
         trans_copy(g).wait()
+
+        def put(value, lane):
+            hi, lo = split(value)
+            tpack[g, pl.ds(0, E), pl.ds(lane, LANES)] = hi
+            tpack[g, pl.ds(EP, E), pl.ds(lane, LANES)] = lo
+
         for m in range(GROUP):
-            hi, lo = split(traw[g * GROUP + m])
-            tpack[g * GROUP + m, pl.ds(0, E), :] = hi
-            tpack[g * GROUP + m, pl.ds(EP, E), :] = lo
+            put(traw[g * GROUP + m, :, pl.ds(0, LANES)], m * LANES)
+        for m in range(0, GROUP, 4):
+            tails = []
+            for k in range(4):
+                tails += [traw[g * GROUP + m + k, :, pl.ds(LANES, E - LANES)], pad]
+            put(jnp.concatenate(tails, axis=1), GROUP * LANES + m * TAIL)
 
     code_copy.wait()
 
-    forwards = []
-    for n in range(2):
-        sends[n].wait_recv()
-        copy = pltpu.make_async_remote_copy(
+    def forward_copy(n):
+        return pltpu.make_async_remote_copy(
             src_ref=halo.at[n, half_rows],
             dst_ref=halo.at[n, half_rows],
             send_sem=fwd_send.at[n],
@@ -177,16 +196,17 @@
             device_id=mate,
             device_id_type=MESH,
         )
-        copy.start()
-        forwards.append(copy)
+
+    forwards = [forward_copy(parity), forward_copy(1 - parity)]
+    for n in range(2):
+        halo_copy(parity if n == 0 else 1 - parity).wait_recv()
+        forwards[n].start()
     for copy in forwards:
         copy.wait_recv()
 
     lane16 = lax.broadcasted_iota(jnp.int32, (16, LANES), 1)
-
-    @pl.loop(0, EP // 16)
-    def _(b):
-        rows = pl.ds(pl.multiple_of(b * 16, 16), 16)
+    for b in range(EP // 16):
+        rows = pl.ds(b * 16, 16)
 
         def tile(ref, q):
             return ref[rows, pl.ds(q * LANES, LANES)]
@@ -199,36 +219,38 @@
             tile(own, 2) + tile(rhalo, 0),
             tile(rhalo, 1),
         ]
-        for s in range(8):
-            shift = LANES - R * s
-            if s == 0:
-                tiles = window
-            else:
-                rolled = [pltpu.roll(w, shift, 1) for w in window]
-                tiles = [jnp.where(lane16 < shift, rolled[q], rolled[q + 1]) for q in range(4)]
-            for q, value in enumerate(tiles):
-                hi, lo = split(value)
-                yhi[s * 5 + q, rows, :] = hi
-                ylo[s * 5 + q, rows, :] = lo
-
-    def step(c, acc):
+        for ref, terms in zip((yhi, ylo), zip(*map(split, window))):
+            for s in range(8):
+                shift = LANES - R * s
+                if s == 0:
+                    tiles = terms
+                else:
+                    rolled = [pltpu.roll(w, shift, 1) for w in terms]
+                    tiles = [jnp.where(lane16 < shift, rolled[q], rolled[q + 1]) for q in range(4)]
+                for q, value in enumerate(tiles):
+                    ref[s * 5 + q, rows, :] = value
+
+    def sources(ref, c):
         begin = codes_s[c, 0]
         at = lax.rem(begin, 8) * 5 + begin // 8
-        mask = masks[c]
-
-        def sources(ref):
-            pieces = [
-                (ref[at + n].reshape(EP // 16, 16, LANES) * mask[None, :, n * LANES : (n + 1) * LANES])
-                .reshape(EP, LANES)
-                for n in range(2)
-            ]
-            return jnp.concatenate(pieces, axis=1)[:E]
-
-        both = jnp.dot(tpack[c], sources(yhi), preferred_element_type=jnp.float32)
-        low = jnp.dot(tpack[c, pl.ds(0, EP), :], sources(ylo), preferred_element_type=jnp.float32)
-        return acc + (both[:EP] + (both[EP:] + low))
-
-    acc = lax.fori_loop(0, classes, step, jnp.zeros((EP, TGT * R), jnp.float32))
+        pieces = []
+        for n in range(2):
+            mask = masks[c, :, pl.ds(n * LANES, LANES)]
+            value = ref[at + n].reshape(EP // 16, 16, LANES) * mask[None]
+            pieces.append(value.reshape(EP, LANES))
+        return jnp.concatenate(pieces, axis=1)
+
+    def stacked(ref, g):
+        values = [sources(ref, g * GROUP + m) for m in range(GROUP)]
+        return jnp.concatenate([v[:LANES] for v in values] + [v[LANES:] for v in values], axis=0)
+
+    acc = jnp.zeros((EP, TGT * R), jnp.float32)
+    for g in range(groups):
+        both = jnp.dot(tpack[g], stacked(yhi, g), preferred_element_type=jnp.float32)
+        low = jnp.dot(
+            tpack[g, pl.ds(0, EP), :], stacked(ylo, g), preferred_element_type=jnp.float32
+        )
+        acc = acc + (both[:EP] + (both[EP:] + low))
 
     lane8 = lax.broadcasted_iota(jnp.int32, (8, LANES), 1)
     for g in range(TILES // 2):
@@ -255,17 +277,18 @@
         finals.append(copy)
     for copy in finals:
         copy.wait_recv()
-    for g in range(TILES // 2):
-        rows = pl.ds(g * 8, 8)
-        total = sendbuf[off, rows, :]
-        for n in (1, 2, 3):
-            total = total + recvbuf[n, rows, :]
-        out_ref[:, pl.ds(2 * g * LANES, LANES)] = block_transpose(total)[: TGT // OFFS]
-        if 2 * g + 1 < E // 8:
-            other = block_transpose(pltpu.roll(total, 64, 1))
-            out_ref[:, pl.ds((2 * g + 1) * LANES, LANES)] = other[: TGT // OFFS]
+    out_ref[...] = (sendbuf[off] + recvbuf[1]) + (recvbuf[2] + recvbuf[3])
     for copy in sends + forwards + finals:
         copy.wait_send()
+
+
+def finish(sum_ref, out_ref):
+    for g in range(TILES // 2):
+        total = sum_ref[pl.ds(g * 8, 8), :]
+        for n in range(2):
+            if 2 * g + n < E // 8:
+                value = block_transpose(total if n == 0 else pltpu.roll(total, 64, 1))
+                out_ref[:, pl.ds((2 * g + n) * LANES, LANES)] = value[: TGT // OFFS]
 
 
 def solution(mesh):
@@ -279,18 +302,19 @@
         def body(*refs):
             kernel(parts, *refs)
 
-        return pl.pallas_call(
+        vmem_spec = pl.BlockSpec(memory_space=pltpu.VMEM)
+        total = pl.pallas_call(
             body,
-            out_shape=jax.ShapeDtypeStruct((TGT // OFFS, E * R), jnp.float32),
+            out_shape=jax.ShapeDtypeStruct((HALF, LANES), jnp.float32),
             in_specs=[any_spec] * 5,
-            out_specs=pl.BlockSpec(memory_space=pltpu.VMEM),
+            out_specs=vmem_spec,
             scratch_shapes=[
                 pltpu.VMEM((SLOTS, TILES * LANES), jnp.float32),
                 pltpu.SMEM((SLOTS,), jnp.int32),
                 pltpu.VMEM(vlist_src.shape, jnp.int32),
                 pltpu.VMEM(vlist_class.shape, jnp.int32),
                 pltpu.VMEM(translation.shape, jnp.float32),
-                pltpu.VMEM((classes, 2 * EP, E), jnp.bfloat16),
+                pltpu.VMEM((classes // GROUP, 2 * EP, GROUP * EP), jnp.bfloat16),
                 pltpu.VMEM((EP, 3 * LANES), jnp.float32),
                 pltpu.VMEM((2, EP, 2 * LANES), jnp.float32),
                 pltpu.VMEM((40, EP, LANES), jnp.bfloat16),
@@ -301,7 +325,7 @@
                 pltpu.SMEM((classes, LANES), jnp.int32),
                 pltpu.VMEM((OFFS, HALF, LANES), jnp.float32),
                 pltpu.VMEM((OFFS, HALF, LANES), jnp.float32),
-                pltpu.SemaphoreType.DMA((4,)),
+                pltpu.SemaphoreType.DMA((5,)),
                 pltpu.SemaphoreType.DMA((classes // GROUP,)),
                 pltpu.SemaphoreType.DMA((2,)),
                 pltpu.SemaphoreType.DMA((2,)),
@@ -313,6 +337,12 @@
             ],
             compiler_params=pltpu.CompilerParams(collective_id=0, has_side_effects=True),
         )(contrib, slot_octant, vlist_src, vlist_class, translation)
+        return pl.pallas_call(
+            finish,
+            out_shape=jax.ShapeDtypeStruct((TGT // OFFS, E * R), jnp.float32),
+            in_specs=[vmem_spec],
+            out_specs=vmem_spec,
+        )(total)
 
     return jax.shard_map(
         local,

time: 38.4 us -> 29 us (0.76)
  Pallas kernels: 36.8 us -> 28.8 us
  local copies, waits for them, and re-layouts: 1.39 us -> 0 us
    pallas_call x1 -> x2, Pallas kernels: 36.8 us -> 28.8 us  [the longest x1 27.1 us: local(): pl.pallas_call(body, out_shape=jax.ShapeDtypeStruct((HALF, LANES), jnp.fl...]
    unnamed x1 -> x0, local copies, waits for them, and re-layouts: 1.39 us -> none
where the time goes in v2:
time: 29 us; the launch traced here: 28.8 us
  Pallas kernels  28.8 us (99%)
    pallas_call x1, Pallas kernels, local(): pl.pallas_call(body, out_shape=jax.ShapeDtypeStruct((HALF, LANES), jnp.fl...  27.1 us
    pallas_call x1, Pallas kernels, local(): pl.pallas_call(finish, out_shape=jax.ShapeDtypeStruct((TGT // OFFS, E * R...  1.69 us

profile of v2, /device:TPU:1, one launch (start us, length us, event | category | flops | bytes accessed | tf_op | source)
XLA Modules:
  0.0 28.8 jit_solution(10217953523976779565)
XLA Ops:
  0.0 27.1 %shard_map.55.sum_ref = f32[80,128]{1,0:T(8,128)} custom-call(f32[24,2432]{1,0:T(8,128)} %refs_0_.1, s32[24]{0:T(128)} %refs_1_.1, s32[16,80]{1,0:T(8,128)} %refs_2_.1, s32[16,80]{1,0:T(8,128)} %refs_3_.1, f32[40,152,152]{2,1,0:T(8,128)} %refs_4_.1), custom_call_target="tpu_custom_call" | custom-call | tf_op jit(solution)/shard_map/pallas_call | solution.py:306
  27.1 1.7 %shard_map.56 = f32[4,2432]{1,0:T(4,128)} custom-call(f32[80,128]{1,0:T(8,128)} %shard_map.55.sum_ref), custom_call_target="tpu_custom_call" | custom-call | tf_op jit(solution)/shard_map/pallas_call | solution.py:340

commit v3 on v2

--- a/solution.py
+++ b/solution.py
@@ -46,7 +46,7 @@
     parts,
     contrib_ref, slot_ref, src_ref, cls_ref, trans_ref, out_ref,
     cbuf, slots, srcv, clsv, traw, tpack,
-    own, halo, yhi, ylo, offs, masks, codes, codes_s,
+    own, halo, ywin, offs, masks, codes, codes_s,
     sendbuf, recvbuf,
     load_sem, trans_sem, halo_send, halo_recv, fwd_send, fwd_recv, code_sem, rs_send, rs_recv,
 ):
@@ -158,7 +158,8 @@
         )
         offs[pl.ds(c, 1), :] = found
         present = jnp.broadcast_to((found > 0.0).astype(jnp.float32), (16, TGT * R))
-        masks[c] = present.astype(jnp.bfloat16)
+        for n in range(2):
+            masks[c, n] = present[:, n * LANES : (n + 1) * LANES].astype(jnp.bfloat16)
 
     start = jnp.max(offs[...], axis=1, keepdims=True).astype(jnp.int32) - 1
     codes[...] = jnp.broadcast_to(jnp.clip(start, 0, 2 * REACH), codes.shape)
@@ -201,71 +202,69 @@
     for n in range(2):
         halo_copy(parity if n == 0 else 1 - parity).wait_recv()
         forwards[n].start()
+
+    lane16 = lax.broadcasted_iota(jnp.int32, (16, LANES), 1)
+    lhalo, rhalo = halo.at[0], halo.at[1]
+
+    def shifted(half):
+        for b in range(HALF // 16):
+            rows = pl.ds(pl.multiple_of(half * HALF, 16) + b * 16, 16)
+
+            def tile(ref, q):
+                return ref[rows, pl.ds(q * LANES, LANES)]
+
+            window = [
+                tile(lhalo, 0),
+                tile(lhalo, 1) + tile(own, 0),
+                tile(own, 1),
+                tile(own, 2) + tile(rhalo, 0),
+                tile(rhalo, 1),
+            ]
+            for k, terms in enumerate(zip(*map(split, window))):
+                for s in range(8):
+                    shift = LANES - R * s
+                    if s == 0:
+                        tiles = terms
+                    else:
+                        rolled = [pltpu.roll(w, shift, 1) for w in terms]
+                        tiles = [
+                            jnp.where(lane16 < shift, rolled[q], rolled[q + 1]) for q in range(4)
+                        ]
+                    for q, value in enumerate(tiles):
+                        ywin[s * 5 + q, rows, pl.ds(k * LANES, LANES)] = value
+
+    shifted(core)
     for copy in forwards:
         copy.wait_recv()
-
-    lane16 = lax.broadcasted_iota(jnp.int32, (16, LANES), 1)
-    for b in range(EP // 16):
-        rows = pl.ds(b * 16, 16)
-
-        def tile(ref, q):
-            return ref[rows, pl.ds(q * LANES, LANES)]
-
-        lhalo, rhalo = halo.at[0], halo.at[1]
-        window = [
-            tile(lhalo, 0),
-            tile(lhalo, 1) + tile(own, 0),
-            tile(own, 1),
-            tile(own, 2) + tile(rhalo, 0),
-            tile(rhalo, 1),
-        ]
-        for ref, terms in zip((yhi, ylo), zip(*map(split, window))):
-            for s in range(8):
-                shift = LANES - R * s
-                if s == 0:
-                    tiles = terms
-                else:
-                    rolled = [pltpu.roll(w, shift, 1) for w in terms]
-                    tiles = [jnp.where(lane16 < shift, rolled[q], rolled[q + 1]) for q in range(4)]
-                for q, value in enumerate(tiles):
-                    ref[s * 5 + q, rows, :] = value
-
-    def sources(ref, c):
-        begin = codes_s[c, 0]
-        at = lax.rem(begin, 8) * 5 + begin // 8
-        pieces = []
-        for n in range(2):
-            mask = masks[c, :, pl.ds(n * LANES, LANES)]
-            value = ref[at + n].reshape(EP // 16, 16, LANES) * mask[None]
-            pieces.append(value.reshape(EP, LANES))
-        return jnp.concatenate(pieces, axis=1)
-
-    def stacked(ref, g):
-        values = [sources(ref, g * GROUP + m) for m in range(GROUP)]
+    shifted(1 - core)
+
+    def stacked(g, n):
+        values = []
+        for c in range(g * GROUP, (g + 1) * GROUP):
+            begin = codes_s[c, 0]
+            at = lax.rem(begin, 8) * 5 + begin // 8
+            mask = masks[c, n]
+            both = jnp.concatenate([mask, mask], axis=1)
+            value = ywin[at + n].reshape(EP // 16, 16, 2 * LANES) * both[None]
+            values.append(value.reshape(EP, 2 * LANES))
         return jnp.concatenate([v[:LANES] for v in values] + [v[LANES:] for v in values], axis=0)
 
-    acc = jnp.zeros((EP, TGT * R), jnp.float32)
-    for g in range(groups):
-        both = jnp.dot(tpack[g], stacked(yhi, g), preferred_element_type=jnp.float32)
-        low = jnp.dot(
-            tpack[g, pl.ds(0, EP), :], stacked(ylo, g), preferred_element_type=jnp.float32
-        )
-        acc = acc + (both[:EP] + (both[EP:] + low))
-
     lane8 = lax.broadcasted_iota(jnp.int32, (8, LANES), 1)
-    for g in range(TILES // 2):
-        for h in range(2):
-            a, b = (
-                acc[(2 * g + n) * 8 : (2 * g + n + 1) * 8, h * LANES : (h + 1) * LANES]
-                for n in range(2)
-            )
+
+    def partial_sums(n):
+        acc = jnp.zeros((EP, LANES), jnp.float32)
+        for g in range(groups):
+            prod = jnp.dot(tpack[g], stacked(g, n), preferred_element_type=jnp.float32)
+            acc = acc + (prod[:EP, :LANES] + (prod[EP:, :LANES] + prod[:EP, LANES:]))
+        for g in range(TILES // 2):
+            a, b = (acc[(2 * g + k) * 8 : (2 * g + k + 1) * 8] for k in range(2))
             rows = pl.ds(g * 8, 8)
-            sendbuf[2 * h, rows, :] = jnp.where(lane8 < 64, a, pltpu.roll(b, 64, 1))
-            sendbuf[2 * h + 1, rows, :] = jnp.where(lane8 < 64, pltpu.roll(a, 64, 1), b)
-    finals = []
-    for n in (2, 3, 1):
-        peer = lax.rem(off + n, OFFS)
-        copy = pltpu.make_async_remote_copy(
+            sendbuf[2 * n, rows, :] = jnp.where(lane8 < 64, a, pltpu.roll(b, 64, 1))
+            sendbuf[2 * n + 1, rows, :] = jnp.where(lane8 < 64, pltpu.roll(a, 64, 1), b)
+
+    def final_copy(peer):
+        n = lax.rem(peer - off + OFFS, OFFS)
+        return pltpu.make_async_remote_copy(
             src_ref=sendbuf.at[peer],
             dst_ref=recvbuf.at[n],
             send_sem=rs_send.at[n - 1],
@@ -273,10 +272,17 @@
             device_id=(dom, peer),
             device_id_type=MESH,
         )
+
+    chip = off // 2
+    partial_sums(1 - chip)
+    finals = [final_copy(2 * (1 - chip) + k) for k in range(2)]
+    for copy in finals:
         copy.start()
-        finals.append(copy)
-    for copy in finals:
-        copy.wait_recv()
+    partial_sums(chip)
+    finals.append(final_copy(2 * chip + 1 - core))
+    finals[2].start()
+    for n in (1, 2, 3):
+        final_copy(lax.rem(off + n, OFFS)).wait_recv()
     out_ref[...] = (sendbuf[off] + recvbuf[1]) + (recvbuf[2] + recvbuf[3])
     for copy in sends + forwards + finals:
         copy.wait_send()
@@ -297,7 +303,10 @@
     def local(contrib, slot_octant, vlist_src, vlist_class, translation):
         classes = translation.shape[0]
         wide = TGT * R
-        any_spec = pl.BlockSpec(memory_space=pl.ANY)
+        hbm_spec = pl.BlockSpec(memory_space=pltpu.HBM)
+
+        args = (contrib, slot_octant, vlist_src, vlist_class, translation)
+        args = [pltpu.with_memory_space_constraint(a, pltpu.HBM) for a in args]
 
         def body(*refs):
             kernel(parts, *refs)
@@ -306,7 +315,7 @@
         total = pl.pallas_call(
             body,
             out_shape=jax.ShapeDtypeStruct((HALF, LANES), jnp.float32),
-            in_specs=[any_spec] * 5,
+            in_specs=[hbm_spec] * 5,
             out_specs=vmem_spec,
             scratch_shapes=[
                 pltpu.VMEM((SLOTS, TILES * LANES), jnp.float32),
@@ -317,10 +326,9 @@
                 pltpu.VMEM((classes // GROUP, 2 * EP, GROUP * EP), jnp.bfloat16),
                 pltpu.VMEM((EP, 3 * LANES), jnp.float32),
                 pltpu.VMEM((2, EP, 2 * LANES), jnp.float32),
-                pltpu.VMEM((40, EP, LANES), jnp.bfloat16),
-                pltpu.VMEM((40, EP, LANES), jnp.bfloat16),
+                pltpu.VMEM((40, EP, 2 * LANES), jnp.bfloat16),
                 pltpu.VMEM((classes, wide), jnp.float32),
-                pltpu.VMEM((classes, 16, wide), jnp.bfloat16),
+                pltpu.VMEM((classes, 2, 16, LANES), jnp.bfloat16),
                 pltpu.VMEM((classes, LANES), jnp.int32),
                 pltpu.SMEM((classes, LANES), jnp.int32),
                 pltpu.VMEM((OFFS, HALF, LANES), jnp.float32),
@@ -335,13 +343,16 @@
                 pltpu.SemaphoreType.DMA((3,)),
                 pltpu.SemaphoreType.DMA((3,)),
             ],
-            compiler_params=pltpu.CompilerParams(collective_id=0, has_side_effects=True),
-        )(contrib, slot_octant, vlist_src, vlist_class, translation)
+            compiler_params=pltpu.CompilerParams(
+                collective_id=0, has_side_effects=True, vmem_limit_bytes=32 << 20
+            ),
+        )(*args)
         return pl.pallas_call(
             finish,
             out_shape=jax.ShapeDtypeStruct((TGT // OFFS, E * R), jnp.float32),
             in_specs=[vmem_spec],
             out_specs=vmem_spec,
+            compiler_params=pltpu.CompilerParams(vmem_limit_bytes=8 << 20),
         )(total)
 
     return jax.shard_map(

time: 29 us -> 26.8 us (0.924)
  Pallas kernels: 28.8 us -> 26.7 us
    pallas_call x1, Pallas kernels: 27.1 us -> 25.8 us  [local(): pl.pallas_call(body, out_shape=jax.ShapeDtypeStruct((HALF, LANES), jnp.fl...]
    pallas_call x1, Pallas kernels: 1.69 us -> 0.91 us  [local(): pl.pallas_call(finish, out_shape=jax.ShapeDtypeStruct((TGT // OFFS, E * R...]
where the time goes in v3:
time: 26.8 us; the launch traced here: 26.7 us
  Pallas kernels  26.7 us (100%)
    pallas_call x1, Pallas kernels, local(): pl.pallas_call(body, out_shape=jax.ShapeDtypeStruct((HALF, LANES), jnp.fl...  25.8 us
    pallas_call x1, Pallas kernels, local(): pl.pallas_call(finish, out_shape=jax.ShapeDtypeStruct((TGT // OFFS, E * R...  0.91 us

profile of v3, /device:TPU:1, one launch (start us, length us, event | category | flops | bytes accessed | tf_op | source)
XLA Modules:
  0.0 26.7 jit_solution(12673488881925583513)
XLA Ops:
  0.0 25.8 %shard_map.55.sum_ref = f32[80,128]{1,0:T(8,128)S(1)} custom-call(f32[24,2432]{1,0:T(8,128)} %refs_0_.1, s32[24]{0:T(128)} %refs_1_.1, s32[16,80]{1,0:T(8,128)} %refs_2_.1, s32[16,80]{1,0:T(8,128)} %refs_3_.1, f32[40,152,152]{2,1,0:T(8,128)} %refs_4_.1), custom_call_target="tpu_custom_call" | custom-call | tf_op jit(solution)/shard_map/pallas_call | solution.py:315
  25.8 0.9 %shard_map.56 = f32[4,2432]{1,0:T(4,128)} custom-call(f32[80,128]{1,0:T(8,128)S(1)} %shard_map.55.sum_ref), custom_call_target="tpu_custom_call" | custom-call | tf_op jit(solution)/shard_map/pallas_call | solution.py:350

commit v4 on v3

--- a/solution.py
+++ b/solution.py
@@ -19,7 +19,6 @@
 OFFS = 4
 GROUP = 8
 WIDE = TILES // 2 * LANES
-TAIL = EP - LANES
 
 
 def block_transpose(v):
@@ -46,7 +45,7 @@
     parts,
     contrib_ref, slot_ref, src_ref, cls_ref, trans_ref, out_ref,
     cbuf, slots, srcv, clsv, traw, tpack,
-    own, halo, ywin, offs, masks, codes, codes_s,
+    own, halo, ywin, xbuf, offs, masks, codes, codes_s,
     sendbuf, recvbuf,
     load_sem, trans_sem, halo_send, halo_recv, fwd_send, fwd_recv, code_sem, rs_send, rs_recv,
 ):
@@ -172,19 +171,17 @@
     @pl.loop(0, groups)
     def _(g):
         trans_copy(g).wait()
-
-        def put(value, lane):
-            hi, lo = split(value)
-            tpack[g, pl.ds(0, E), pl.ds(lane, LANES)] = hi
-            tpack[g, pl.ds(EP, E), pl.ds(lane, LANES)] = lo
-
-        for m in range(GROUP):
-            put(traw[g * GROUP + m, :, pl.ds(0, LANES)], m * LANES)
-        for m in range(0, GROUP, 4):
-            tails = []
-            for k in range(4):
-                tails += [traw[g * GROUP + m + k, :, pl.ds(LANES, E - LANES)], pad]
-            put(jnp.concatenate(tails, axis=1), GROUP * LANES + m * TAIL)
+        lanes = pl.ds(pl.multiple_of(g * (GROUP * HALF), LANES), GROUP * HALF)
+        for half in range(2):
+            pieces = []
+            for m in range(GROUP):
+                if half == 0:
+                    pieces.append(traw[g * GROUP + m, :, pl.ds(0, HALF)])
+                else:
+                    pieces += [traw[g * GROUP + m, :, pl.ds(HALF, E - HALF)], pad]
+            for k, term in enumerate(split(jnp.concatenate(pieces, axis=1))):
+                tpack[half, pl.ds(k * HALF, HALF), lanes] = term[:HALF]
+                tpack[half, pl.ds(EP + k * HALF, E - HALF), lanes] = term[HALF:]
 
     code_copy.wait()
 
@@ -233,56 +230,84 @@
                     for q, value in enumerate(tiles):
                         ywin[s * 5 + q, rows, pl.ds(k * LANES, LANES)] = value
 
-    shifted(core)
-    for copy in forwards:
-        copy.wait_recv()
-    shifted(1 - core)
-
-    def stacked(g, n):
+    def stacked(half, n, chunk):
         values = []
-        for c in range(g * GROUP, (g + 1) * GROUP):
+        for c in range(chunk.start, chunk.stop):
             begin = codes_s[c, 0]
             at = lax.rem(begin, 8) * 5 + begin // 8
             mask = masks[c, n]
             both = jnp.concatenate([mask, mask], axis=1)
-            value = ywin[at + n].reshape(EP // 16, 16, 2 * LANES) * both[None]
-            values.append(value.reshape(EP, 2 * LANES))
-        return jnp.concatenate([v[:LANES] for v in values] + [v[LANES:] for v in values], axis=0)
+            rows = pl.ds(pl.multiple_of(half * HALF, 16), HALF)
+            value = ywin[at + n, rows, :].reshape(HALF // 16, 16, 2 * LANES) * both[None]
+            values.append(value.reshape(HALF, 2 * LANES))
+        return jnp.concatenate(values, axis=0)
+
+    def product(half, part, chunk, sources):
+        lanes = pl.ds(chunk.start * HALF, len(chunk) * HALF)
+        prod = jnp.dot(
+            tpack[half, pl.ds(part * EP, EP), lanes], sources, preferred_element_type=jnp.float32
+        )
+        return prod[:HALF, :LANES] + (prod[HALF:, :LANES] + prod[:HALF, LANES:])
+
+    chunks = [range(c, min(c + 2 * GROUP, classes)) for c in range(0, classes, 2 * GROUP)]
+
+    def whole_product(half, n, sums):
+        for chunk in chunks:
+            value = stacked(half, n, chunk)
+            sums = [sums[part] + product(half, part, chunk, value) for part in range(2)]
+        return sums
 
     lane8 = lax.broadcasted_iota(jnp.int32, (8, LANES), 1)
 
-    def partial_sums(n):
-        acc = jnp.zeros((EP, LANES), jnp.float32)
-        for g in range(groups):
-            prod = jnp.dot(tpack[g], stacked(g, n), preferred_element_type=jnp.float32)
-            acc = acc + (prod[:EP, :LANES] + (prod[EP:, :LANES] + prod[:EP, LANES:]))
-        for g in range(TILES // 2):
-            a, b = (acc[(2 * g + k) * 8 : (2 * g + k + 1) * 8] for k in range(2))
-            rows = pl.ds(g * 8, 8)
+    def to_send(n, part, value):
+        for g in range(HALF // 16):
+            a, b = (value[(2 * g + k) * 8 : (2 * g + k + 1) * 8] for k in range(2))
+            rows = pl.ds((part * (HALF // 16) + g) * 8, 8)
             sendbuf[2 * n, rows, :] = jnp.where(lane8 < 64, a, pltpu.roll(b, 64, 1))
             sendbuf[2 * n + 1, rows, :] = jnp.where(lane8 < 64, pltpu.roll(a, 64, 1), b)
 
-    def final_copy(peer):
+    def final_copy(peer, part):
         n = lax.rem(peer - off + OFFS, OFFS)
+        rows = pl.ds(part * (HALF // 2), HALF // 2)
         return pltpu.make_async_remote_copy(
-            src_ref=sendbuf.at[peer],
-            dst_ref=recvbuf.at[n],
-            send_sem=rs_send.at[n - 1],
-            recv_sem=rs_recv.at[n - 1],
+            src_ref=sendbuf.at[peer, rows],
+            dst_ref=recvbuf.at[n, rows],
+            send_sem=rs_send.at[n - 1, part],
+            recv_sem=rs_recv.at[n - 1, part],
             device_id=(dom, peer),
             device_id_type=MESH,
         )
 
     chip = off // 2
-    partial_sums(1 - chip)
-    finals = [final_copy(2 * (1 - chip) + k) for k in range(2)]
-    for copy in finals:
-        copy.start()
-    partial_sums(chip)
-    finals.append(final_copy(2 * chip + 1 - core))
-    finals[2].start()
+    zero = jnp.zeros((HALF, LANES), jnp.float32)
+    shifted(core)
+    sums = whole_product(core, 1 - chip, [zero, zero])
+    for copy in forwards:
+        copy.wait_recv()
+    shifted(1 - core)
+    finals = []
+    for part in range(2):
+        for chunk in chunks:
+            rows = pl.ds(chunk.start * HALF, len(chunk) * HALF)
+            if part == 0:
+                value = stacked(1 - core, 1 - chip, chunk)
+                xbuf[rows, :] = value
+            else:
+                value = xbuf[rows, :]
+            sums[part] = sums[part] + product(1 - core, part, chunk, value)
+        to_send(1 - chip, part, sums[part])
+        for k in range(2):
+            finals.append(final_copy(2 * (1 - chip) + k, part))
+            finals[-1].start()
+    sums = whole_product(core, chip, [zero, zero])
+    sums = whole_product(1 - core, chip, sums)
+    for part in range(2):
+        to_send(chip, part, sums[part])
+        finals.append(final_copy(2 * chip + 1 - core, part))
+        finals[-1].start()
     for n in (1, 2, 3):
-        final_copy(lax.rem(off + n, OFFS)).wait_recv()
+        for part in range(2):
+            final_copy(lax.rem(off + n, OFFS), part).wait_recv()
     out_ref[...] = (sendbuf[off] + recvbuf[1]) + (recvbuf[2] + recvbuf[3])
     for copy in sends + forwards + finals:
         copy.wait_send()
@@ -323,10 +348,11 @@
                 pltpu.VMEM(vlist_src.shape, jnp.int32),
                 pltpu.VMEM(vlist_class.shape, jnp.int32),
                 pltpu.VMEM(translation.shape, jnp.float32),
-                pltpu.VMEM((classes // GROUP, 2 * EP, GROUP * EP), jnp.bfloat16),
+                pltpu.VMEM((2, 2 * EP, classes * HALF), jnp.bfloat16),
                 pltpu.VMEM((EP, 3 * LANES), jnp.float32),
                 pltpu.VMEM((2, EP, 2 * LANES), jnp.float32),
                 pltpu.VMEM((40, EP, 2 * LANES), jnp.bfloat16),
+                pltpu.VMEM((classes * HALF, 2 * LANES), jnp.bfloat16),
                 pltpu.VMEM((classes, wide), jnp.float32),
                 pltpu.VMEM((classes, 2, 16, LANES), jnp.bfloat16),
                 pltpu.VMEM((classes, LANES), jnp.int32),
@@ -340,8 +366,8 @@
                 pltpu.SemaphoreType.DMA((2,)),
                 pltpu.SemaphoreType.DMA((2,)),
                 pltpu.SemaphoreType.DMA(()),
-                pltpu.SemaphoreType.DMA((3,)),
-                pltpu.SemaphoreType.DMA((3,)),
+                pltpu.SemaphoreType.DMA((3, 2)),
+                pltpu.SemaphoreType.DMA((3, 2)),
             ],
             compiler_params=pltpu.CompilerParams(
                 collective_id=0, has_side_effects=True, vmem_limit_bytes=32 << 20

time: 26.8 us -> 26.8 us (level)
  no operation moved by 1% of the time
where the time goes in v4:
time: 26.8 us; the launch traced here: 26.7 us
  Pallas kernels  26.7 us (100%)
    pallas_call x1, Pallas kernels, local(): pl.pallas_call(body, out_shape=jax.ShapeDtypeStruct((HALF, LANES), jnp.fl...  25.7 us
    pallas_call x1, Pallas kernels, local(): pl.pallas_call(finish, out_shape=jax.ShapeDtypeStruct((TGT // OFFS, E * R...  0.91 us

profile of v4, /device:TPU:1, one launch (start us, length us, event | category | flops | bytes accessed | tf_op | source)
XLA Modules:
  0.0 26.7 jit_solution(1282518411405239704)
XLA Ops:
  0.0 25.7 %shard_map.55.sum_ref = f32[80,128]{1,0:T(8,128)S(1)} custom-call(f32[24,2432]{1,0:T(8,128)} %refs_0_.1, s32[24]{0:T(128)} %refs_1_.1, s32[16,80]{1,0:T(8,128)} %refs_2_.1, s32[16,80]{1,0:T(8,128)} %refs_3_.1, f32[40,152,152]{2,1,0:T(8,128)} %refs_4_.1), custom_call_target="tpu_custom_call" | custom-call | tf_op jit(solution)/shard_map/pallas_call | solution.py:340
  25.7 0.9 %shard_map.56 = f32[4,2432]{1,0:T(4,128)} custom-call(f32[80,128]{1,0:T(8,128)S(1)} %shard_map.55.sum_ref), custom_call_target="tpu_custom_call" | custom-call | tf_op jit(solution)/shard_map/pallas_call | solution.py:376

commit v5 on v3

--- a/solution.py
+++ b/solution.py
@@ -18,8 +18,8 @@
 TILES = 20
 OFFS = 4
 GROUP = 8
+CHUNKS = ((0, 48), (48, 32))
 WIDE = TILES // 2 * LANES
-TAIL = EP - LANES
 
 
 def block_transpose(v):
@@ -53,7 +53,6 @@
     dom = lax.axis_index("dom")
     off = lax.axis_index("off")
     core = lax.rem(off, 2)
-    parity = lax.rem(dom, 2)
     octants = TGT * parts
     classes = trans_ref.shape[0]
     groups = classes // GROUP
@@ -93,8 +92,8 @@
         for s in range(SLOTS - TGT)
     ]
 
-    def own_half(half):
-        for n in range(TILES // 2):
+    def own_half(half, first_point, points_count):
+        for n in range(first_point // 8, (first_point + points_count) // 8):
             lanes = pl.ds(pl.multiple_of(half * WIDE, LANES) + n * LANES, LANES)
             points = pl.ds(pl.multiple_of(half * HALF, 8) + n * 8, 8)
             first = pltpu.roll(cbuf[pl.ds(0, 8), lanes], 4, 0)
@@ -111,28 +110,29 @@
             for b in range(3):
                 own[points, pl.ds(b * LANES, LANES)] = block_transpose(table[b])
 
-    own_half(core)
-    pl.semaphore_wait(barrier, len(peers))
-
-    half_rows = pl.ds(pl.multiple_of(core * HALF, HALF), HALF)
-
-    def halo_copy(n):
+    def halo_copy(n, k):
+        first_point, count = CHUNKS[k]
+        rows = pl.ds(pl.multiple_of(core * HALF, HALF) + first_point, count)
         return pltpu.make_async_remote_copy(
-            src_ref=own.at[half_rows, pl.ds(pl.multiple_of((1 - n) * LANES, LANES), 2 * LANES)],
-            dst_ref=halo.at[n, half_rows],
-            send_sem=halo_send.at[n],
-            recv_sem=halo_recv.at[n],
-            device_id=(lax.rem(dom + 1 + n * (parts - 2), parts), across),
+            src_ref=own.at[rows, pl.ds((1 - n) * LANES, 2 * LANES)],
+            dst_ref=halo.at[n, rows],
+            send_sem=halo_send.at[n, k],
+            recv_sem=halo_recv.at[n, k],
+            device_id=(lax.rem(dom + (1 if n == 0 else parts - 1), parts), across),
             device_id_type=MESH,
         )
 
-    sends = [halo_copy(1 - parity), halo_copy(parity)]
-    for copy in sends:
+    own_half(core, *CHUNKS[0])
+    pl.semaphore_wait(barrier, len(peers))
+    sends = [halo_copy(n, k) for n in range(2) for k in range(2)]
+    sends[0].start()
+    own_half(core, *CHUNKS[1])
+    for copy in sends[1:]:
         copy.start()
     for g in range(groups):
         trans_copy(g).start()
     loads[2].wait()
-    own_half(1 - core)
+    own_half(1 - core, 0, HALF)
 
     loads[3].wait()
     loads[4].wait()
@@ -167,47 +167,48 @@
     code_copy.start()
 
     tpack[...] = jnp.zeros(tpack.shape, jnp.bfloat16)
-    pad = jnp.zeros((E, EP - E), jnp.float32)
 
     @pl.loop(0, groups)
     def _(g):
         trans_copy(g).wait()
-
-        def put(value, lane):
-            hi, lo = split(value)
-            tpack[g, pl.ds(0, E), pl.ds(lane, LANES)] = hi
-            tpack[g, pl.ds(EP, E), pl.ds(lane, LANES)] = lo
-
-        for m in range(GROUP):
-            put(traw[g * GROUP + m, :, pl.ds(0, LANES)], m * LANES)
-        for m in range(0, GROUP, 4):
-            tails = []
-            for k in range(4):
-                tails += [traw[g * GROUP + m + k, :, pl.ds(LANES, E - LANES)], pad]
-            put(jnp.concatenate(tails, axis=1), GROUP * LANES + m * TAIL)
+        for half in range(2):
+            for first_point, count in CHUNKS:
+                begin = half * HALF + first_point
+                size = min(begin + count, E) - begin
+                pieces = []
+                for m in range(GROUP):
+                    pieces.append(traw[g * GROUP + m, :, pl.ds(begin, size)])
+                    if size < count:
+                        pieces.append(jnp.zeros((E, count - size), jnp.float32))
+                lanes = pl.ds(
+                    pl.multiple_of(classes * first_point + g * (GROUP * count), LANES),
+                    GROUP * count,
+                )
+                for k, term in enumerate(split(jnp.concatenate(pieces, axis=1))):
+                    tpack[half, pl.ds(k * EP, E), lanes] = term
 
     code_copy.wait()
 
-    def forward_copy(n):
+    def forward_copy(n, k):
+        first_point, count = CHUNKS[k]
+        rows = pl.ds(pl.multiple_of(core * HALF, HALF) + first_point, count)
         return pltpu.make_async_remote_copy(
-            src_ref=halo.at[n, half_rows],
-            dst_ref=halo.at[n, half_rows],
-            send_sem=fwd_send.at[n],
-            recv_sem=fwd_recv.at[n],
+            src_ref=halo.at[n, rows],
+            dst_ref=halo.at[n, rows],
+            send_sem=fwd_send.at[n, k],
+            recv_sem=fwd_recv.at[n, k],
             device_id=mate,
             device_id_type=MESH,
         )
 
-    forwards = [forward_copy(parity), forward_copy(1 - parity)]
-    for n in range(2):
-        halo_copy(parity if n == 0 else 1 - parity).wait_recv()
-        forwards[n].start()
+    forwards = [[forward_copy(n, k) for n in range(2)] for k in range(2)]
 
     lane16 = lax.broadcasted_iota(jnp.int32, (16, LANES), 1)
     lhalo, rhalo = halo.at[0], halo.at[1]
 
-    def shifted(half):
-        for b in range(HALF // 16):
+    def shifted(half, k):
+        first_point, count = CHUNKS[k]
+        for b in range(first_point // 16, (first_point + count) // 16):
             rows = pl.ds(pl.multiple_of(half * HALF, 16) + b * 16, 16)
 
             def tile(ref, q):
@@ -220,7 +221,7 @@
                 tile(own, 2) + tile(rhalo, 0),
                 tile(rhalo, 1),
             ]
-            for k, terms in enumerate(zip(*map(split, window))):
+            for term, terms in enumerate(zip(*map(split, window))):
                 for s in range(8):
                     shift = LANES - R * s
                     if s == 0:
@@ -231,33 +232,38 @@
                             jnp.where(lane16 < shift, rolled[q], rolled[q + 1]) for q in range(4)
                         ]
                     for q, value in enumerate(tiles):
-                        ywin[s * 5 + q, rows, pl.ds(k * LANES, LANES)] = value
-
-    shifted(core)
-    for copy in forwards:
-        copy.wait_recv()
-    shifted(1 - core)
-
-    def stacked(g, n):
+                        ywin[s * 5 + q, rows, pl.ds(term * LANES, LANES)] = value
+
+    def stacked(half, k, n, chosen):
+        first_point, count = CHUNKS[k]
+        rows = pl.ds(pl.multiple_of(half * HALF, 16) + first_point, count)
         values = []
-        for c in range(g * GROUP, (g + 1) * GROUP):
+        for c in chosen:
             begin = codes_s[c, 0]
             at = lax.rem(begin, 8) * 5 + begin // 8
             mask = masks[c, n]
             both = jnp.concatenate([mask, mask], axis=1)
-            value = ywin[at + n].reshape(EP // 16, 16, 2 * LANES) * both[None]
-            values.append(value.reshape(EP, 2 * LANES))
-        return jnp.concatenate([v[:LANES] for v in values] + [v[LANES:] for v in values], axis=0)
+            value = ywin[at + n, rows, :].reshape(count // 16, 16, 2 * LANES) * both[None]
+            values.append(value.reshape(count, 2 * LANES))
+        return jnp.concatenate(values, axis=0)
+
+    def product(half, k, n, total):
+        first_point, count = CHUNKS[k]
+        for c in range(0, classes, 2 * GROUP):
+            chosen = range(c, min(c + 2 * GROUP, classes))
+            lanes = pl.ds(classes * first_point + c * count, len(chosen) * count)
+            prod = jnp.dot(
+                tpack[half, :, lanes], stacked(half, k, n, chosen),
+                preferred_element_type=jnp.float32,
+            )
+            total = total + (prod[:EP, :LANES] + (prod[EP:, :LANES] + prod[:EP, LANES:]))
+        return total
 
     lane8 = lax.broadcasted_iota(jnp.int32, (8, LANES), 1)
 
-    def partial_sums(n):
-        acc = jnp.zeros((EP, LANES), jnp.float32)
-        for g in range(groups):
-            prod = jnp.dot(tpack[g], stacked(g, n), preferred_element_type=jnp.float32)
-            acc = acc + (prod[:EP, :LANES] + (prod[EP:, :LANES] + prod[:EP, LANES:]))
+    def to_send(n, value):
         for g in range(TILES // 2):
-            a, b = (acc[(2 * g + k) * 8 : (2 * g + k + 1) * 8] for k in range(2))
+            a, b = (value[(2 * g + k) * 8 : (2 * g + k + 1) * 8] for k in range(2))
             rows = pl.ds(g * 8, 8)
             sendbuf[2 * n, rows, :] = jnp.where(lane8 < 64, a, pltpu.roll(b, 64, 1))
             sendbuf[2 * n + 1, rows, :] = jnp.where(lane8 < 64, pltpu.roll(a, 64, 1), b)
@@ -274,17 +280,33 @@
         )
 
     chip = off // 2
-    partial_sums(1 - chip)
+    total = jnp.zeros((EP, LANES), jnp.float32)
+    for k in range(2):
+        for n in range(2):
+            sends[2 * n + k].wait_recv()
+            forwards[k][n].start()
+        shifted(core, k)
+        total = product(core, k, 1 - chip, total)
+    for k in range(2):
+        for copy in forwards[k]:
+            copy.wait_recv()
+        shifted(1 - core, k)
+        total = product(1 - core, k, 1 - chip, total)
+    to_send(1 - chip, total)
     finals = [final_copy(2 * (1 - chip) + k) for k in range(2)]
     for copy in finals:
         copy.start()
-    partial_sums(chip)
+    total = jnp.zeros((EP, LANES), jnp.float32)
+    for half in range(2):
+        for k in range(2):
+            total = product(half, k, chip, total)
+    to_send(chip, total)
     finals.append(final_copy(2 * chip + 1 - core))
     finals[2].start()
     for n in (1, 2, 3):
         final_copy(lax.rem(off + n, OFFS)).wait_recv()
     out_ref[...] = (sendbuf[off] + recvbuf[1]) + (recvbuf[2] + recvbuf[3])
-    for copy in sends + forwards + finals:
+    for copy in sends + forwards[0] + forwards[1] + finals:
         copy.wait_send()
 
 
@@ -323,7 +345,7 @@
                 pltpu.VMEM(vlist_src.shape, jnp.int32),
                 pltpu.VMEM(vlist_class.shape, jnp.int32),
                 pltpu.VMEM(translation.shape, jnp.float32),
-                pltpu.VMEM((classes // GROUP, 2 * EP, GROUP * EP), jnp.bfloat16),
+                pltpu.VMEM((2, 2 * EP, classes * HALF), jnp.bfloat16),
                 pltpu.VMEM((EP, 3 * LANES), jnp.float32),
                 pltpu.VMEM((2, EP, 2 * LANES), jnp.float32),
                 pltpu.VMEM((40, EP, 2 * LANES), jnp.bfloat16),
@@ -335,10 +357,10 @@
                 pltpu.VMEM((OFFS, HALF, LANES), jnp.float32),
                 pltpu.SemaphoreType.DMA((5,)),
                 pltpu.SemaphoreType.DMA((classes // GROUP,)),
-                pltpu.SemaphoreType.DMA((2,)),
-                pltpu.SemaphoreType.DMA((2,)),
-                pltpu.SemaphoreType.DMA((2,)),
-                pltpu.SemaphoreType.DMA((2,)),
+                pltpu.SemaphoreType.DMA((2, 2)),
+                pltpu.SemaphoreType.DMA((2, 2)),
+                pltpu.SemaphoreType.DMA((2, 2)),
+                pltpu.SemaphoreType.DMA((2, 2)),
                 pltpu.SemaphoreType.DMA(()),
                 pltpu.SemaphoreType.DMA((3,)),
                 pltpu.SemaphoreType.DMA((3,)),

time: 26.8 us -> 28.2 us (1.052)
  Pallas kernels: 26.7 us -> 28.1 us
    pallas_call x1, Pallas kernels: 25.8 us -> 27.2 us  [local(): pl.pallas_call(body, out_shape=jax.ShapeDtypeStruct((HALF, LANES), jnp.fl...]
where the time goes in v5:
time: 28.2 us; the launch traced here: 28.1 us
  Pallas kernels  28.1 us (100%)
    pallas_call x1, Pallas kernels, local(): pl.pallas_call(body, out_shape=jax.ShapeDtypeStruct((HALF, LANES), jnp.fl...  27.2 us
    pallas_call x1, Pallas kernels, local(): pl.pallas_call(finish, out_shape=jax.ShapeDtypeStruct((TGT // OFFS, E * R...  0.91 us

profile of v5, /device:TPU:1, one launch (start us, length us, event | category | flops | bytes accessed | tf_op | source)
XLA Modules:
  0.0 28.1 jit_solution(400082872312386220)
XLA Ops:
  0.0 27.2 %shard_map.55.sum_ref = f32[80,128]{1,0:T(8,128)S(1)} custom-call(f32[24,2432]{1,0:T(8,128)} %refs_0_.1, s32[24]{0:T(128)} %refs_1_.1, s32[16,80]{1,0:T(8,128)} %refs_2_.1, s32[16,80]{1,0:T(8,128)} %refs_3_.1, f32[40,152,152]{2,1,0:T(8,128)} %refs_4_.1), custom_call_target="tpu_custom_call" | custom-call | tf_op jit(solution)/shard_map/pallas_call | solution.py:337
  27.2 0.9 %shard_map.56 = f32[4,2432]{1,0:T(4,128)} custom-call(f32[80,128]{1,0:T(8,128)S(1)} %shard_map.55.sum_ref), custom_call_target="tpu_custom_call" | custom-call | tf_op jit(solution)/shard_map/pallas_call | solution.py:372

commit v6 on v5

--- a/solution.py
+++ b/solution.py
@@ -18,7 +18,7 @@
 TILES = 20
 OFFS = 4
 GROUP = 8
-CHUNKS = ((0, 48), (48, 32))
+CHUNKS = ((0, HALF),)
 WIDE = TILES // 2 * LANES
 
 
@@ -82,6 +82,9 @@
     def trans_copy(g):
         rows = pl.ds(g * GROUP, GROUP)
         return pltpu.make_async_copy(trans_ref.at[rows], traw.at[rows], trans_sem.at[g])
+
+    for g in range(groups):
+        trans_copy(g).start()
 
     cbuf[:, pl.ds(E * R, LANES)] = jnp.zeros((SLOTS, LANES), jnp.float32)
     row = lax.broadcasted_iota(jnp.int32, (8, LANES), 0)
@@ -122,72 +125,72 @@
             device_id_type=MESH,
         )
 
-    own_half(core, *CHUNKS[0])
+    def prepare():
+        loads[2].wait()
+        own_half(1 - core, 0, HALF)
+
+        loads[3].wait()
+        loads[4].wait()
+        target = lax.broadcasted_iota(jnp.int32, srcv.shape, 0) + dom * TGT
+        code = lax.rem(srcv[...] - target + (REACH + octants), octants) + 1
+        spread = (
+            lax.broadcasted_iota(jnp.int32, (TGT, TGT * R), 0)
+            == lax.broadcasted_iota(jnp.int32, (TGT, TGT * R), 1) // R
+        ).astype(jnp.float32)
+        dims = (((0,), (0,)), ((), ()))
+        code_l = lax.dot_general(
+            code.astype(jnp.float32), spread, dims, preferred_element_type=jnp.float32
+        )
+        class_l = lax.dot_general(
+            (clsv[...] - off * classes).astype(jnp.float32), spread, dims,
+            preferred_element_type=jnp.float32,
+        )
+
+        @pl.loop(0, classes)
+        def _(c):
+            found = jnp.max(
+                jnp.where(class_l == c.astype(jnp.float32), code_l, 0.0), axis=0, keepdims=True
+            )
+            offs[pl.ds(c, 1), :] = found
+            present = jnp.broadcast_to((found > 0.0).astype(jnp.float32), (16, TGT * R))
+            for n in range(2):
+                masks[c, n] = present[:, n * LANES : (n + 1) * LANES].astype(jnp.bfloat16)
+
+        start = jnp.max(offs[...], axis=1, keepdims=True).astype(jnp.int32) - 1
+        codes[...] = jnp.broadcast_to(jnp.clip(start, 0, 2 * REACH), codes.shape)
+        code_copy = pltpu.make_async_copy(codes, codes_s, code_sem)
+        code_copy.start()
+
+        tpack[...] = jnp.zeros(tpack.shape, jnp.bfloat16)
+
+        @pl.loop(0, groups)
+        def _(g):
+            trans_copy(g).wait()
+            for half in range(2):
+                for first_point, count in CHUNKS:
+                    begin = half * HALF + first_point
+                    size = min(begin + count, E) - begin
+                    pieces = []
+                    for m in range(GROUP):
+                        pieces.append(traw[g * GROUP + m, :, pl.ds(begin, size)])
+                        if size < count:
+                            pieces.append(jnp.zeros((E, count - size), jnp.float32))
+                    lanes = pl.ds(
+                        pl.multiple_of(classes * first_point + g * (GROUP * count), LANES),
+                        GROUP * count,
+                    )
+                    for k, term in enumerate(split(jnp.concatenate(pieces, axis=1))):
+                        tpack[half, pl.ds(k * EP, E), lanes] = term
+
+        code_copy.wait()
+
+    own_half(core, 0, HALF)
+    pl.when(dom == 0)(prepare)
     pl.semaphore_wait(barrier, len(peers))
-    sends = [halo_copy(n, k) for n in range(2) for k in range(2)]
-    sends[0].start()
-    own_half(core, *CHUNKS[1])
-    for copy in sends[1:]:
+    sends = [halo_copy(n, 0) for n in range(2)]
+    for copy in sends:
         copy.start()
-    for g in range(groups):
-        trans_copy(g).start()
-    loads[2].wait()
-    own_half(1 - core, 0, HALF)
-
-    loads[3].wait()
-    loads[4].wait()
-    target = lax.broadcasted_iota(jnp.int32, srcv.shape, 0) + dom * TGT
-    code = lax.rem(srcv[...] - target + (REACH + octants), octants) + 1
-    spread = (
-        lax.broadcasted_iota(jnp.int32, (TGT, TGT * R), 0)
-        == lax.broadcasted_iota(jnp.int32, (TGT, TGT * R), 1) // R
-    ).astype(jnp.float32)
-    dims = (((0,), (0,)), ((), ()))
-    code_l = lax.dot_general(
-        code.astype(jnp.float32), spread, dims, preferred_element_type=jnp.float32
-    )
-    class_l = lax.dot_general(
-        (clsv[...] - off * classes).astype(jnp.float32), spread, dims,
-        preferred_element_type=jnp.float32,
-    )
-
-    @pl.loop(0, classes)
-    def _(c):
-        found = jnp.max(
-            jnp.where(class_l == c.astype(jnp.float32), code_l, 0.0), axis=0, keepdims=True
-        )
-        offs[pl.ds(c, 1), :] = found
-        present = jnp.broadcast_to((found > 0.0).astype(jnp.float32), (16, TGT * R))
-        for n in range(2):
-            masks[c, n] = present[:, n * LANES : (n + 1) * LANES].astype(jnp.bfloat16)
-
-    start = jnp.max(offs[...], axis=1, keepdims=True).astype(jnp.int32) - 1
-    codes[...] = jnp.broadcast_to(jnp.clip(start, 0, 2 * REACH), codes.shape)
-    code_copy = pltpu.make_async_copy(codes, codes_s, code_sem)
-    code_copy.start()
-
-    tpack[...] = jnp.zeros(tpack.shape, jnp.bfloat16)
-
-    @pl.loop(0, groups)
-    def _(g):
-        trans_copy(g).wait()
-        for half in range(2):
-            for first_point, count in CHUNKS:
-                begin = half * HALF + first_point
-                size = min(begin + count, E) - begin
-                pieces = []
-                for m in range(GROUP):
-                    pieces.append(traw[g * GROUP + m, :, pl.ds(begin, size)])
-                    if size < count:
-                        pieces.append(jnp.zeros((E, count - size), jnp.float32))
-                lanes = pl.ds(
-                    pl.multiple_of(classes * first_point + g * (GROUP * count), LANES),
-                    GROUP * count,
-                )
-                for k, term in enumerate(split(jnp.concatenate(pieces, axis=1))):
-                    tpack[half, pl.ds(k * EP, E), lanes] = term
-
-    code_copy.wait()
+    pl.when(dom != 0)(prepare)
 
     def forward_copy(n, k):
         first_point, count = CHUNKS[k]
@@ -201,12 +204,12 @@
             device_id_type=MESH,
         )
 
-    forwards = [[forward_copy(n, k) for n in range(2)] for k in range(2)]
+    forwards = [[forward_copy(n, k) for n in range(2)] for k in range(len(CHUNKS))]
 
     lane16 = lax.broadcasted_iota(jnp.int32, (16, LANES), 1)
     lhalo, rhalo = halo.at[0], halo.at[1]
 
-    def shifted(half, k):
+    def shifted(half, k, left):
         first_point, count = CHUNKS[k]
         for b in range(first_point // 16, (first_point + count) // 16):
             rows = pl.ds(pl.multiple_of(half * HALF, 16) + b * 16, 16)
@@ -214,25 +217,24 @@
             def tile(ref, q):
                 return ref[rows, pl.ds(q * LANES, LANES)]
 
-            window = [
-                tile(lhalo, 0),
-                tile(lhalo, 1) + tile(own, 0),
-                tile(own, 1),
-                tile(own, 2) + tile(rhalo, 0),
-                tile(rhalo, 1),
-            ]
+            if left:
+                first_tile = 0
+                window = [tile(lhalo, 0), tile(lhalo, 1) + tile(own, 0), tile(own, 1)]
+            else:
+                first_tile = 2
+                window = [tile(own, 1), tile(own, 2) + tile(rhalo, 0), tile(rhalo, 1)]
             for term, terms in enumerate(zip(*map(split, window))):
                 for s in range(8):
                     shift = LANES - R * s
                     if s == 0:
-                        tiles = terms
+                        tiles = terms[:2] if left else terms
                     else:
                         rolled = [pltpu.roll(w, shift, 1) for w in terms]
                         tiles = [
-                            jnp.where(lane16 < shift, rolled[q], rolled[q + 1]) for q in range(4)
+                            jnp.where(lane16 < shift, rolled[q], rolled[q + 1]) for q in range(2)
                         ]
                     for q, value in enumerate(tiles):
-                        ywin[s * 5 + q, rows, pl.ds(term * LANES, LANES)] = value
+                        ywin[s * 5 + first_tile + q, rows, pl.ds(term * LANES, LANES)] = value
 
     def stacked(half, k, n, chosen):
         first_point, count = CHUNKS[k]
@@ -281,24 +283,22 @@
 
     chip = off // 2
     total = jnp.zeros((EP, LANES), jnp.float32)
-    for k in range(2):
-        for n in range(2):
-            sends[2 * n + k].wait_recv()
-            forwards[k][n].start()
-        shifted(core, k)
-        total = product(core, k, 1 - chip, total)
-    for k in range(2):
-        for copy in forwards[k]:
-            copy.wait_recv()
-        shifted(1 - core, k)
-        total = product(1 - core, k, 1 - chip, total)
+    for n in (1, 0):
+        sends[n].wait_recv()
+        forwards[0][n].start()
+        shifted(core, 0, n == 0)
+        if n == 0:
+            total = product(core, 0, 1 - chip, total)
+        forwards[0][n].wait_recv()
+        shifted(1 - core, 0, n == 0)
+    total = product(1 - core, 0, 1 - chip, total)
     to_send(1 - chip, total)
-    finals = [final_copy(2 * (1 - chip) + k) for k in range(2)]
+    finals = [final_copy(2 * (1 - chip) + k) for k in (1, 0)]
     for copy in finals:
         copy.start()
     total = jnp.zeros((EP, LANES), jnp.float32)
     for half in range(2):
-        for k in range(2):
+        for k in range(len(CHUNKS)):
             total = product(half, k, chip, total)
     to_send(chip, total)
     finals.append(final_copy(2 * chip + 1 - core))
@@ -306,17 +306,17 @@
     for n in (1, 2, 3):
         final_copy(lax.rem(off + n, OFFS)).wait_recv()
     out_ref[...] = (sendbuf[off] + recvbuf[1]) + (recvbuf[2] + recvbuf[3])
-    for copy in sends + forwards[0] + forwards[1] + finals:
+    for copy in sends + forwards[0] + finals:
         copy.wait_send()
 
 
 def finish(sum_ref, out_ref):
     for g in range(TILES // 2):
-        total = sum_ref[pl.ds(g * 8, 8), :]
+        value = block_transpose(sum_ref[pl.ds(g * 8, 8), :])
         for n in range(2):
             if 2 * g + n < E // 8:
-                value = block_transpose(total if n == 0 else pltpu.roll(total, 64, 1))
-                out_ref[:, pl.ds((2 * g + n) * LANES, LANES)] = value[: TGT // OFFS]
+                rows = value[n * TGT // OFFS : (n + 1) * TGT // OFFS]
+                out_ref[:, pl.ds((2 * g + n) * LANES, LANES)] = rows
 
 
 def solution(mesh):

time: 28.2 us -> 25.9 us (0.918)
  Pallas kernels: 28.1 us -> 25.8 us
    pallas_call x1, Pallas kernels: 27.2 us -> 24.9 us  [local(): pl.pallas_call(body, out_shape=jax.ShapeDtypeStruct((HALF, LANES), jnp.fl...]
where the time goes in v6:
time: 25.9 us; the launch traced here: 25.8 us
  Pallas kernels  25.8 us (100%)
    pallas_call x1, Pallas kernels, local(): pl.pallas_call(body, out_shape=jax.ShapeDtypeStruct((HALF, LANES), jnp.fl...  24.9 us
    pallas_call x1, Pallas kernels, local(): pl.pallas_call(finish, out_shape=jax.ShapeDtypeStruct((TGT // OFFS, E * R...  0.85 us

profile of v6, /device:TPU:1, one launch (start us, length us, event | category | flops | bytes accessed | tf_op | source)
XLA Modules:
  0.0 25.8 jit_solution(16313266756886644321)
XLA Ops:
  0.0 24.9 %shard_map.55.sum_ref = f32[80,128]{1,0:T(8,128)S(1)} custom-call(f32[24,2432]{1,0:T(8,128)} %refs_0_.1, s32[24]{0:T(128)} %refs_1_.1, s32[16,80]{1,0:T(8,128)} %refs_2_.1, s32[16,80]{1,0:T(8,128)} %refs_3_.1, f32[40,152,152]{2,1,0:T(8,128)} %refs_4_.1), custom_call_target="tpu_custom_call" | custom-call | tf_op jit(solution)/shard_map/pallas_call | solution.py:337
  25.0 0.8 %shard_map.56 = f32[4,2432]{1,0:T(4,128)} custom-call(f32[80,128]{1,0:T(8,128)S(1)} %shard_map.55.sum_ref), custom_call_target="tpu_custom_call" | custom-call | tf_op jit(solution)/shard_map/pallas_call | solution.py:372

commit v7 on v6

--- a/solution.py
+++ b/solution.py
@@ -305,18 +305,17 @@
     finals[2].start()
     for n in (1, 2, 3):
         final_copy(lax.rem(off + n, OFFS)).wait_recv()
-    out_ref[...] = (sendbuf[off] + recvbuf[1]) + (recvbuf[2] + recvbuf[3])
+    for g in range(TILES // 2):
+        rows = pl.ds(g * 8, 8)
+        value = block_transpose(
+            (sendbuf[off, rows, :] + recvbuf[1, rows, :]) + (recvbuf[2, rows, :] + recvbuf[3, rows, :])
+        )
+        for n in range(2):
+            if 2 * g + n < E // 8:
+                part = value[n * TGT // OFFS : (n + 1) * TGT // OFFS]
+                out_ref[:, pl.ds((2 * g + n) * LANES, LANES)] = part
     for copy in sends + forwards[0] + finals:
         copy.wait_send()
-
-
-def finish(sum_ref, out_ref):
-    for g in range(TILES // 2):
-        value = block_transpose(sum_ref[pl.ds(g * 8, 8), :])
-        for n in range(2):
-            if 2 * g + n < E // 8:
-                rows = value[n * TGT // OFFS : (n + 1) * TGT // OFFS]
-                out_ref[:, pl.ds((2 * g + n) * LANES, LANES)] = rows
 
 
 def solution(mesh):
@@ -336,7 +335,7 @@
         vmem_spec = pl.BlockSpec(memory_space=pltpu.VMEM)
         total = pl.pallas_call(
             body,
-            out_shape=jax.ShapeDtypeStruct((HALF, LANES), jnp.float32),
+            out_shape=jax.ShapeDtypeStruct((TGT // OFFS, E * R), jnp.float32),
             in_specs=[hbm_spec] * 5,
             out_specs=vmem_spec,
             scratch_shapes=[
@@ -369,13 +368,7 @@
                 collective_id=0, has_side_effects=True, vmem_limit_bytes=32 << 20
             ),
         )(*args)
-        return pl.pallas_call(
-            finish,
-            out_shape=jax.ShapeDtypeStruct((TGT // OFFS, E * R), jnp.float32),
-            in_specs=[vmem_spec],
-            out_specs=vmem_spec,
-            compiler_params=pltpu.CompilerParams(vmem_limit_bytes=8 << 20),
-        )(total)
+        return total
 
     return jax.shard_map(
         local,

time: 25.9 us -> 25.9 us (level)
  local copies, waits for them, and re-layouts: 0 us -> 0.62 us
  Pallas kernels: 25.8 us -> 25.2 us
    pallas_call x2 -> x1, Pallas kernels: 25.8 us -> 25.2 us  [local(): pl.pallas_call(body, out_shape=jax.ShapeDtypeStruct((TGT // OFFS, E * R),...]
    unnamed x0 -> x1, local copies, waits for them, and re-layouts: none -> 0.62 us
where the time goes in v7:
time: 25.9 us; the launch traced here: 25.8 us
  Pallas kernels  25.2 us (97%)
  local copies, waits for them, and re-layouts  0.62 us (2%)
    pallas_call x1, Pallas kernels, local(): pl.pallas_call(body, out_shape=jax.ShapeDtypeStruct((TGT // OFFS, E * R),...  25.2 us
    unnamed x1, local copies, waits for them, and re-layouts  0.62 us

profile of v7, /device:TPU:1, one launch (start us, length us, event | category | flops | bytes accessed | tf_op | source)
XLA Modules:
  0.0 25.8 jit_solution(17142734882934498228)
XLA Ops:
  0.0 25.2 %shard_map.55 = f32[4,2432]{1,0:T(4,128)S(1)} custom-call(f32[24,2432]{1,0:T(8,128)} %refs_0_.1, s32[24]{0:T(128)} %refs_1_.1, s32[16,80]{1,0:T(8,128)} %refs_2_.1, s32[16,80]{1,0:T(8,128)} %refs_3_.1, f32[40,152,152]{2,1,0:T(8,128)} %refs_4_.1), custom_call_target="tpu_custom_call" | custom-call | tf_op jit(solution)/shard_map/pallas_call | solution.py:336
  25.2 0.6 %copy.7 = f32[4,2432]{1,0:T(4,128)} copy(f32[4,2432]{1,0:T(4,128)S(1)} %shard_map.55) | data formatting | bytes 77824
